TPU v7x, 1024 devices: a whole 4x8x16 slice. The times are simulated.
1024 devices in a mesh: section: 4 (over x), ctx: 16 (over y, core), exp: 16 (over z).
Axes of the slice: x: 4, y: 8, z: 16, core: 2. Of those that a mesh axis runs over, the one named last changes fastest.
Arguments:
- queries: bfloat16 [16384, 8192], P('ctx', ('section', 'exp')), may hold values from -6 to 6
- key_rows: bfloat16 [16384, 8192], P('ctx', ('section', 'exp')), may hold values from -0.5 to 0.5
- value_rows: bfloat16 [16384, 8192], P('ctx', ('section', 'exp')), may hold values from -6 to 6
- gate_input: bfloat16 [16384, 8192], P('ctx', ('section', 'exp')), may hold values from -6 to 6
- norm_gain: float32 [8192], P(('section', 'exp')), may hold values from 0.25 to 1.75
- log_decay: float32 [64, 16384], P(('section', 'exp'), 'ctx'), may hold values from -1 to 0, as said below
- grad_output: bfloat16 [16384, 8192], P('ctx', ('section', 'exp')), may hold values from -6 to 6
Outputs:
- layer_out: bfloat16 [16384, 8192], P('ctx', ('section', 'exp'))
- grad_queries: bfloat16 [16384, 8192], P('ctx', ('section', 'exp'))
- grad_keys: bfloat16 [16384, 8192], P('ctx', ('section', 'exp'))
- grad_values: bfloat16 [16384, 8192], P('ctx', ('section', 'exp'))
- grad_gate: bfloat16 [16384, 8192], P('ctx', ('section', 'exp'))
Inputs may be any that keep to these rules, and one draw needn't show every extreme that they name: `log_decay`: each entry is the logarithm of one head's decay factor at one position.
All inputs are finite; a program needn't handle non-finite values.
Results may differ from a plain program's by a relative error of at most 0.0051.
Values sent between devices are 32-bit elements; how exact they have to be, the bound alone decides.
No kernel may reach another device: no remote copies, remote signals or barrier semaphores. Data moves between devices by JAX's collectives and lax.ppermute only.
A program may use at most 32 MiB of HBM per device.

v0:
```python
from functools import partial

import jax
import jax.numpy as jnp
from jax import lax
from jax.sharding import PartitionSpec as P

HEAD_DIM = 128


precise = lax.Precision.HIGHEST
epsilon = 1e-06


def entering_2(part, axis, combine, identity, reverse):
    count = lax.axis_size(axis)
    place = lax.axis_index(axis)
    ahead = count - 1 - place if reverse else place
    gathered = jax.tree.map(lambda a: lax.all_gather(a, axis), part)
    state = jax.tree.map(lambda a, e: jnp.zeros_like(a) + jnp.asarray(e, a.dtype), part, identity)

    def one(turn, state):
        source = count - 1 - turn if reverse else turn
        return combine(
            state, jax.tree.map(lambda a: lax.dynamic_index_in_dim(a, source, 0, False), gathered)
        )

    return lax.fori_loop(0, ahead, one, state)


def decay_weights(log_rates):
    cumulated = jnp.cumsum(log_rates)
    length = log_rates.shape[0]
    row_index = lax.broadcasted_iota(jnp.int32, (length, length), 0)
    col_index = lax.broadcasted_iota(jnp.int32, (length, length), 1)
    lower = jnp.exp(jnp.minimum(cumulated[:, None] - cumulated[None, :], 0.0))
    return (cumulated, jnp.where(row_index >= col_index, lower, 0.0))


def block_forward(entering, pieces):
    queries, key_rows, value_rows, log_rates = pieces
    cumulated, weights_table = decay_weights(log_rates)
    scores = jnp.dot(queries, key_rows.T, preferred_element_type=jnp.float32)
    weights = (scores * weights_table).astype(jnp.bfloat16)
    carried = jnp.dot(queries.astype(jnp.float32), entering, precision=precise)
    output = (
        jnp.dot(weights, value_rows, preferred_element_type=jnp.float32)
        + jnp.exp(cumulated)[:, None] * carried
    )
    tail_decay = jnp.exp(cumulated[-1] - cumulated)[:, None]
    update = jnp.dot(
        (key_rows.astype(jnp.float32) * tail_decay).T,
        value_rows.astype(jnp.float32),
        precision=precise,
    )
    leaving = jnp.exp(cumulated[-1]) * entering + update
    return (leaving, (output, entering))


def split_blocks(tensor, block_len):
    return tensor.reshape((tensor.shape[0] // block_len, block_len) + tensor.shape[1:])


def forward_run(queries, key_rows, value_rows, log_rates, start, block_len):
    pieces = tuple((split_blocks(t, block_len) for t in (queries, key_rows, value_rows, log_rates)))
    closing, (outputs, entries) = lax.scan(block_forward, start, pieces)
    return (outputs.reshape(queries.shape), entries, closing)


def block_backward(leaving, pieces):
    queries, key_rows, value_rows, grad_attn, log_rates, entering = pieces
    cumulated, weights_table = decay_weights(log_rates)
    qk_weights = (
        jnp.dot(queries, key_rows.T, preferred_element_type=jnp.float32) * weights_table
    ).astype(jnp.bfloat16)
    dv_weights = (
        jnp.dot(grad_attn, value_rows.T, preferred_element_type=jnp.float32) * weights_table
    ).astype(jnp.bfloat16)
    front_decay = jnp.exp(cumulated)[:, None]
    tail_decay = jnp.exp(cumulated[-1] - cumulated)[:, None]
    grad_float = grad_attn.astype(jnp.float32)
    grad_q = jnp.dot(
        dv_weights, key_rows, preferred_element_type=jnp.float32
    ) + front_decay * jnp.dot(grad_float, entering.T, precision=precise)
    grad_k = jnp.dot(
        dv_weights.T, queries, preferred_element_type=jnp.float32
    ) + tail_decay * jnp.dot(value_rows.astype(jnp.float32), leaving.T, precision=precise)
    grad_v = jnp.dot(
        qk_weights.T, grad_attn, preferred_element_type=jnp.float32
    ) + tail_decay * jnp.dot(key_rows.astype(jnp.float32), leaving, precision=precise)
    arriving = jnp.exp(cumulated[-1]) * leaving + jnp.dot(
        (queries.astype(jnp.float32) * front_decay).T, grad_float, precision=precise
    )
    return (arriving, (grad_q, grad_k, grad_v))


def backward_run(queries, key_rows, value_rows, grad_attn, log_rates, entries, start, block_len):
    pieces = tuple(
        (split_blocks(t, block_len) for t in (queries, key_rows, value_rows, grad_attn, log_rates))
    ) + (entries,)
    closing, (grad_q, grad_k, grad_v) = lax.scan(block_backward, start, pieces, reverse=True)
    shape = queries.shape
    return (grad_q.reshape(shape), grad_k.reshape(shape), grad_v.reshape(shape), closing)


def join_forward(earlier, later_part):
    return (
        jnp.exp(later_part[1])[:, None, None] * earlier[0] + later_part[0],
        earlier[1] + later_part[1],
    )


def join_backward(earlier, later_part):
    return (
        later_part[0] + jnp.exp(later_part[1])[:, None, None] * earlier[0],
        earlier[1] + later_part[1],
    )


def by_heads(tensor, head_count):
    return tensor.reshape(tensor.shape[0], head_count, HEAD_DIM).transpose(1, 0, 2)


def from_heads(tensor):
    return tensor.transpose(1, 0, 2).reshape(tensor.shape[1], tensor.shape[0] * tensor.shape[2])


def on_device(queries, key_rows, value_rows, gate_input, norm_gain, log_decay, grad_output):
    length = queries.shape[0]
    head_count = log_decay.shape[0]
    block_len = min(512, length)
    total_width = head_count * HEAD_DIM * lax.axis_size(("section", "exp"))
    zero_state = jnp.zeros((head_count, HEAD_DIM, HEAD_DIM), jnp.float32)
    zero_totals = jnp.zeros((head_count,), jnp.float32)
    query_heads = by_heads(queries, head_count)
    key_heads = by_heads(key_rows, head_count)
    value_heads = by_heads(value_rows, head_count)
    local_out, entries, local_state = jax.vmap(partial(forward_run, block_len=block_len))(
        query_heads, key_heads, value_heads, log_decay, zero_state
    )
    totals = jnp.sum(log_decay, axis=1)
    cumulated = jnp.cumsum(log_decay, axis=1)
    incoming, passed = entering_2(
        (local_state, totals), "ctx", join_forward, (zero_state, zero_totals), False
    )
    front_decay = jnp.exp(cumulated)[..., None]
    attn_heads = local_out + front_decay * jnp.einsum(
        "hti,hij->htj", query_heads.astype(jnp.float32), incoming, precision=precise
    )
    full_out = from_heads(attn_heads)
    gate_prob = jax.nn.sigmoid(gate_input.astype(jnp.float32))
    grad_float = grad_output.astype(jnp.float32)
    signal = grad_float * gate_prob * norm_gain
    squares = lax.psum(jnp.sum(full_out * full_out, axis=1), ("section", "exp"))
    inv_rms = lax.rsqrt(squares / total_width + epsilon)
    normed = full_out * inv_rms[:, None]
    along = lax.psum(jnp.sum(signal * normed, axis=1), ("section", "exp")) / total_width
    scaled = normed * norm_gain
    layer_out = (scaled * gate_prob).astype(jnp.bfloat16)
    grad_gate = (grad_float * scaled * gate_prob * (1.0 - gate_prob)).astype(jnp.bfloat16)
    grad_attn = (inv_rms[:, None] * (signal - normed * along[:, None])).astype(jnp.bfloat16)
    grad_heads = by_heads(grad_attn, head_count)
    local_q, local_k, local_v, local_back = jax.vmap(partial(backward_run, block_len=block_len))(
        query_heads, key_heads, value_heads, grad_heads, log_decay, entries, zero_state
    )
    later_state, passed_back = entering_2(
        (local_back, totals), "ctx", join_backward, (zero_state, zero_totals), True
    )
    tail_decay = jnp.exp(totals[:, None] - cumulated)[..., None]
    grad_q = local_q + front_decay * jnp.einsum(
        "htj,hij->hti", grad_heads.astype(jnp.float32), incoming, precision=precise
    )
    grad_k = local_k + tail_decay * jnp.einsum(
        "htj,hij->hti", value_heads.astype(jnp.float32), later_state, precision=precise
    )
    grad_v = local_v + tail_decay * jnp.einsum(
        "hti,hij->htj", key_heads.astype(jnp.float32), later_state, precision=precise
    )
    return (
        layer_out,
        from_heads(grad_q).astype(jnp.bfloat16),
        from_heads(grad_k).astype(jnp.bfloat16),
        from_heads(grad_v).astype(jnp.bfloat16),
        grad_gate,
    )


def solution(mesh):
    in_specs = (
        P("ctx", ("section", "exp")),
        P("ctx", ("section", "exp")),
        P("ctx", ("section", "exp")),
        P("ctx", ("section", "exp")),
        P(("section", "exp")),
        P(("section", "exp"), "ctx"),
        P("ctx", ("section", "exp")),
    )
    out_specs = (
        P("ctx", ("section", "exp")),
        P("ctx", ("section", "exp")),
        P("ctx", ("section", "exp")),
        P("ctx", ("section", "exp")),
        P("ctx", ("section", "exp")),
    )
    return jax.shard_map(
        on_device, mesh=mesh, in_specs=in_specs, out_specs=out_specs, check_vma=False
    )
```

profile of v0, /device:TPU:1, one launch (start us, length us, event | category | flops | bytes accessed | tf_op | source)
XLA Modules:
  0.0 477.8 jit_solution(16653750691952158081)
XLA Ops:
  8.3 9.4 %while.64 = (s32[]{:T(128)}, f32[1,128,128]{2,1,0:T(8,128)S(1)}, f32[2,1,512,128]{3,2,1,0:T(8,128)S(1)}, f32[2,1,128,128]{3,2,1,0:T(8,128)S(1)}, f32[2,1,512]{2,...) while((s32[]{:T(128)}, f32[1,128,128]{2,1,0:T(8,128)S(1)}, ...), condition=%wide.region_3.4_spmd.clone, body=%wide.region_0.3_spmd.clone.sunk | while | flops 337527296 | bytes 2981717 | solution.py:66
  24.4 37.1 %all-reduce = f32[16]{0:T(128)S(1)} all-reduce(f32[16]{0:T(128)S(1)} %dynamic-update-slice), channel_id=1, replica_groups=mesh['section'=4,'ctx'=16,'exp'=16] {'ctx'}, use_global_device_ids=true, to_apply=%add | all-reduce | flops 16 | bytes 128
  62.9 10.8 %all-gather.5.cloned.1.call-done = f32[16,128,128]{2,1,0:T(8,128)} async-done(((f32[1,128,128]{2,1,0:T(8,128)}), f32[16,128,128]{2,1,0:T(8,128)}) %all-gather.5.cloned.1.call-update) | async-done | bytes 1048592 | tf_op jit(solution)/shard_map/all_gather | solution.py:19
  73.6 2.1 while.62
  74.2 1.5 bitcast_add_fusion.9
  76.7 117.9 %psum.14 = f32[1024]{0:T(1024)S(1)} all-reduce(f32[1024]{0:T(1024)S(1)} %get-tuple-element.614), channel_id=1, replica_groups=mesh['section'=4,'ctx'=16,'exp'=16] {'section','exp'}, use_global_device_ids=true, to_apply=%region_10.11 | all-reduce | flops 1024 | bytes 8192 | tf_op jit(solution)/shard_map/psum | solution.py:154
  195.6 110.6 %psum.15 = f32[1024]{0:T(1024)S(1)} all-reduce(f32[1024]{0:T(1024)S(1)} %multiply_reduce_fusion), channel_id=1, replica_groups=mesh['section'=4,'ctx'=16,'exp'=16] {'section','exp'}, use_global_device_ids=true, to_apply=%region_12.13 | all-reduce | flops 1024 | bytes 8192 | tf_op jit(solution)/shard_map/psum | solution.py:157
  308.5 14.8 %while.65 = (s32[]{:T(128)}, f32[1,128,128]{2,1,0:T(8,128)S(1)}, f32[2,1,512,128]{3,2,1,0:T(8,128)S(1)}, f32[2,1,512,128]{3,2,1,0:T(8,128)S(1)}, f32[2,1,512,128...) while((s32[]{:T(128)}, f32[1,128,128]{2,1,0:T(8,128)S(1)}, ...), condition=%wide.region_16.17_spmd.clone, body=%wide.region_13.16_spmd.clone.sunk | while | flops 742015488 | bytes 5877603 | solution.py:101
  327.9 110.2 %all-gather.7.cloned.1.call-done = f32[16,128,128]{2,1,0:T(8,128)} async-done(((f32[1,128,128]{2,1,0:T(8,128)}), f32[16,128,128]{2,1,0:T(8,128)}) %all-gather.7.cloned.1.call-update) | async-done | bytes 1048592 | tf_op jit(solution)/shard_map/all_gather | solution.py:19
  438.8 29.7 %while.63 = (s32[]{:T(128)}, f32[1,128,128]{2,1,0:T(8,128)S(1)}, s32[]{:T(128)}, f32[16,1,128,128]{3,2,1,0:T(8,128)}, f32[16,1]{0,1:T(1,128)S(1)}, /*index=5*/s32[]{:T(128)}, s32[]{:T(128)}, s32[]{:T(128)}, s32[]{:T(128)}) while((s32[]{:T(128)}, f32[1,128,128]{2,1,0:T(8,128)S(1)}, s32[]{:T(128)}, f32[16,1,128,128]{3,2,1,0:T(8,128)}, ...), condition=%wide.region_18.19_spmd, body=%wide.region_17.18_spmd.sunk | while | flops 32774 | bytes 196767 | solution.py:28
  439.4 1.5 bitcast_add_fusion.10
  441.5 1.5 bitcast_add_fusion.10
  443.6 1.5 bitcast_add_fusion.10
  445.7 1.5 bitcast_add_fusion.10
  447.9 1.5 bitcast_add_fusion.10
  450.0 1.5 bitcast_add_fusion.10
  452.1 1.5 bitcast_add_fusion.10
  454.2 1.5 bitcast_add_fusion.10
  456.4 1.5 bitcast_add_fusion.10
  458.5 1.5 bitcast_add_fusion.10
  460.6 1.5 bitcast_add_fusion.10
  462.7 1.5 bitcast_add_fusion.10
  464.8 1.5 bitcast_add_fusion.10
  467.0 1.5 bitcast_add_fusion.10
  (156 shorter events, 48.2 us)
Async XLA Ops:
  7.2 66.5 %all-gather.5.cloned.1.call-start = ((), (), s32[]{:S(2)}) async-start(), calls=%async_computation | async-start | bytes 1114112 | tf_op jit(solution)/shard_map/all_gather | solution.py:19
  7.2 0.7 copy-start.10
  7.2 1.0 copy-start
  7.3 1.0 copy-start.1
  8.3 1.1 copy-start.4
  13.0 1.1 copy-start.4
  17.7 0.6 copy-start.3
  17.7 1.3 copy-start.7
  18.4 419.8 %all-gather.7.cloned.1.call-start = ((), (), s32[]{:S(2)}) async-start(), calls=%async_computation.1 | async-start | bytes 1114112 | tf_op jit(solution)/shard_map/all_gather | solution.py:19
  19.0 1.0 copy-start.8
  20.0 0.9 copy-start.9
  62.9 13.4 %copy-start.12 = (f32[1024]{0:T(1024)}, f32[1024]{0:T(1024)S(1)}, u32[]{:S(2)}) copy-start(f32[1024]{0:T(1024)S(1)} %get-tuple-element.613) | copy-start | bytes 12292
  75.7 0.5 copy-start.15
  194.7 0.7 copy-start.14
  307.5 1.0 copy-start.5
  323.3 0.6 copy-start.2
  324.1 1.0 copy-start.6
  325.9 0.8 copy-start.13
  438.2 0.6 copy-start.16
  438.8 29.7 %copy-start.11 = (f32[1024]{0:T(1024)S(1)}, f32[1024]{0:T(1024)}, u32[]{:S(2)}) copy-start(f32[1024]{0:T(1024)} %get-tuple-element.612) | copy-start | bytes 12292
Sparse Core Ops, SparseCore 0:
  18.5 55.1 all-gather.4
  324.0 114.1 all-gather.6
where the time goes:
time: 480 us; the launch traced here: 478 us
  blocking collectives  266 us (55%)
  waiting for transfers between devices  121 us (25%)
  local copies, waits for them, and re-layouts  29.5 us (6%)
  other arithmetic  28.5 us (6%)
  between operations  14.3 us (3%)
  matrix products  12.7 us (3%)
  loops' own time  6.11 us (1%)
    all_gather x2, waiting for transfers between devices, entering_2(): gathered = jax.tree.map(lambda a: lax.all_gather(a, axis), part)  121 us
    psum x1, blocking collectives, on_device(): squares = lax.psum(jnp.sum(full_out * full_out, axis=1), ('section', 'exp'))  118 us
    psum x1, blocking collectives, on_device(): lax.psum(jnp.sum(signal * normed, axis=1), ('section', 'exp')) / total_width  111 us
    unnamed x1, blocking collectives  37.1 us
    add x14, other arithmetic, join_backward(): later_part[0] + jnp.exp(later_part[1])[:, None, None] * earlier[0]  21.1 us
    unnamed x42, local copies, waits for them, and re-layouts  13.7 us
  transfers between devices with their start and end apart: 2, of which 2 were waited for; matrix products, arithmetic and copies ran while one was open for 2% of the time, Pallas kernels for 0%

commit v1 on v0

v1 whole, which is shorter than its diff:
```python
from functools import partial

import jax
import jax.numpy as jnp
from jax import lax
from jax.experimental import pallas as pl
from jax.experimental.pallas import tpu as pltpu
from jax.sharding import PartitionSpec as P

HEAD_DIM = 128
BLOCK = 512
TILE = 256
CHUNK = 128
EPSILON = 1e-06
f32 = jnp.float32
bf16 = jnp.bfloat16


def dot(a, b, ca=1, cb=0):
    return lax.dot_general(a, b, (((ca,), (cb,)), ((), ())), preferred_element_type=f32)


def split3(x):
    hi = x.astype(bf16)
    rest = x - hi.astype(f32)
    mid = rest.astype(bf16)
    return hi, mid, (rest - mid.astype(f32)).astype(bf16)


def exact_dot(a, b, ca=1, cb=0):
    hi, mid, lo = split3(b)
    return dot(a, hi, ca, cb) + (dot(a, mid, ca, cb) + dot(a, lo, ca, cb))


def cumulate(rates):
    rows = rates.shape[0]
    per_block = BLOCK // CHUNK
    r = lax.broadcasted_iota(jnp.int32, (CHUNK, CHUNK), 0)
    c = lax.broadcasted_iota(jnp.int32, (CHUNK, CHUNK), 1)
    upper = jnp.where(r <= c, 1.0, 0.0).astype(bf16)
    hi, mid, lo = split3(rates)
    within = dot(hi, upper) + (dot(mid, upper) + dot(lo, upper))
    total = within[:, CHUNK - 1 :]
    pieces = []
    for row in range(rows):
        value = within[row : row + 1, :]
        for earlier in range(row // per_block * per_block, row):
            value = value + total[earlier : earlier + 1, :]
        pieces.append(value)
    return jnp.concatenate(pieces, axis=0)


def column(turned, first, count):
    return jnp.concatenate(
        [turned[:, r : r + 1] for r in range(first // CHUNK, (first + count) // CHUNK)], axis=0
    )


def row_of(sums, first, count):
    return jnp.concatenate(
        [sums[r : r + 1, :] for r in range(first // CHUNK, (first + count) // CHUNK)], axis=1
    )


def last_of(sums, block):
    row = (block + 1) * BLOCK // CHUNK - 1
    return sums[row : row + 1, CHUNK - 1 :]


def weights_tile(sums, turned, start, tile):
    first = start + tile * TILE
    width = (tile + 1) * TILE
    gap = column(turned, first, TILE) - row_of(sums, start, width)
    lower = jnp.exp(jnp.minimum(gap, 0.0))
    t = lax.broadcasted_iota(jnp.int32, (TILE, width), 0) + tile * TILE
    s = lax.broadcasted_iota(jnp.int32, (TILE, width), 1)
    return jnp.where(t >= s, lower, 0.0)


def states_kernel(n_ctx, k_ref, v_ref, rates_ref, send_ref, entry_ref, sums_ref, turned_ref):
    length = k_ref.shape[0]
    blocks = length // BLOCK
    sums = cumulate(rates_ref[...])
    turned = sums.T
    sums_ref[...] = sums
    turned_ref[...] = turned
    state = None
    total = jnp.zeros((1, 1), f32)
    for b in range(blocks):
        at = b * BLOCK
        last = last_of(sums, b)
        tail = jnp.exp(last - column(turned, at, BLOCK))
        scaled = v_ref[at : at + BLOCK, :].astype(f32) * tail
        update = exact_dot(k_ref[at : at + BLOCK, :], scaled, 0, 0)
        state = update if state is None else jnp.exp(last) * state + update
        total = total + last
        if b < blocks - 1:
            entry_ref[b] = state
    rows = HEAD_DIM // n_ctx
    spread = jnp.broadcast_to(total, (rows, HEAD_DIM))
    for j in range(n_ctx):
        send_ref[j, :rows, :] = state[j * rows : (j + 1) * rows, :]
        send_ref[j, rows:, :] = spread


def prefix_kernel(n_ctx, got_ref, send_ref, totals_ref):
    rows = HEAD_DIM // n_ctx
    state = jnp.zeros((rows, HEAD_DIM), f32)
    for j in range(n_ctx):
        send_ref[j] = state
        total = got_ref[j, rows:, :]
        totals_ref[j] = total
        state = jnp.exp(total) * state + got_ref[j, :rows, :]


def suffix_kernel(n_ctx, got_ref, totals_ref, send_ref):
    rows = HEAD_DIM // n_ctx
    state = jnp.zeros((rows, HEAD_DIM), f32)
    for j in reversed(range(n_ctx)):
        send_ref[j] = state
        state = jnp.exp(totals_ref[j]) * state + got_ref[j]


def local_kernel(q_ref, k_ref, v_ref, sums_ref, turned_ref, out_ref):
    length = q_ref.shape[0]
    sums, turned = sums_ref[...], turned_ref[...]
    for b in range(length // BLOCK):
        at = b * BLOCK
        for i in range(BLOCK // TILE):
            rows = slice(at + i * TILE, at + (i + 1) * TILE)
            cols = slice(at, at + (i + 1) * TILE)
            scores = dot(q_ref[rows, :], k_ref[cols, :], 1, 1)
            weights = (scores * weights_tile(sums, turned, at, i)).astype(bf16)
            out_ref[rows, :] = dot(weights, v_ref[cols, :])


def gate_kernel(gate_ref, grad_ref, gain_ref, prob_ref, signal_ref):
    prob = jax.nn.sigmoid(gate_ref[...].astype(f32))
    prob_ref[...] = prob
    signal_ref[...] = grad_ref[...].astype(f32) * prob * gain_ref[...]


def row_sums(x):
    ones = jnp.ones((8, HEAD_DIM), bf16)
    flat = exact_dot(ones, x, 1, 1)
    rows = x.shape[0] // CHUNK
    at = lax.broadcasted_iota(jnp.int32, (rows, CHUNK), 0)
    out = flat[:, :CHUNK]
    for r in range(1, rows):
        out = jnp.where(at == r, flat[:, r * CHUNK : (r + 1) * CHUNK], out)
    return out


def attn_kernel(
    n_exp, q_ref, local_ref, state_ref, entry_ref, sums_ref, turned_ref, signal_ref,
    attn_ref, entries_ref, send_ref,
):
    length = q_ref.shape[0]
    sums, turned = sums_ref[...], turned_ref[...]
    state = state_ref[...]
    for b in range(length // BLOCK):
        at = b * BLOCK
        rows = slice(at, at + BLOCK)
        if b:
            state = entry_ref[b - 1] + jnp.exp(last) * state_ref[...]
        entries_ref[b] = state
        front = jnp.exp(column(turned, at, BLOCK))
        attn_ref[rows, :] = local_ref[rows, :] + front * exact_dot(q_ref[rows, :], state)
        last = last_of(sums, b) + (last if b else 0.0)
    attn = attn_ref[...]
    squares = row_sums(attn * attn)
    dots = row_sums(signal_ref[...] * attn)
    for j in range(n_exp):
        send_ref[j, :8, :] = squares
        send_ref[j, 8:, :] = dots


def relay_kernel(n_exp, n_section, got_ref, send_ref):
    total = got_ref[0]
    for j in range(1, n_exp):
        total = total + got_ref[j]
    for j in range(n_section):
        send_ref[j] = total


def grad_kernel(
    n_section, width, n_ctx, got_ref, attn_ref, signal_ref, q_ref, sums_ref, turned_ref,
    grad_ref, send_ref, arrive_ref, inverse_ref,
):
    length = q_ref.shape[0]
    sums, turned = sums_ref[...], turned_ref[...]
    total = got_ref[0]
    for j in range(1, n_section):
        total = total + got_ref[j]
    inverse = lax.rsqrt(total[:8] / width + EPSILON)
    along = inverse * total[8:] / width
    both = jnp.concatenate([inverse, along], axis=0).T
    inverse_ref[...] = both
    state = None
    for b in reversed(range(length // BLOCK)):
        at = b * BLOCK
        rows = slice(at, at + BLOCK)
        inv = column(both[:, :8], at, BLOCK)
        alo = column(both[:, 8:], at, BLOCK)
        normed = attn_ref[rows, :] * inv
        grad = (inv * (signal_ref[rows, :] - normed * alo)).astype(bf16)
        grad_ref[rows, :] = grad
        front = jnp.exp(column(turned, at, BLOCK))
        update = exact_dot(q_ref[rows, :], grad.astype(f32) * front, 0, 0)
        if state is None:
            state = update
            if b:
                arrive_ref[b - 1] = state
        else:
            state = jnp.exp(last_of(sums, b)) * state + update
            if b:
                arrive_ref[b - 1] = state
    part = HEAD_DIM // n_ctx
    for j in range(n_ctx):
        send_ref[j] = state[j * part : (j + 1) * part, :]


def output_kernel(
    attn_ref, inverse_ref, prob_ref, gain_ref, gout_ref, layer_ref, gate_ref,
):
    length = attn_ref.shape[0]
    both = inverse_ref[...]
    for b in range(length // BLOCK):
        at = b * BLOCK
        rows = slice(at, at + BLOCK)
        scaled = attn_ref[rows, :] * column(both[:, :8], at, BLOCK) * gain_ref[...]
        prob = prob_ref[rows, :]
        layer = scaled * prob
        layer_ref[rows, :] = layer.astype(bf16)
        gate_ref[rows, :] = (gout_ref[rows, :].astype(f32) * layer * (1.0 - prob)).astype(bf16)


def backward_kernel(
    q_ref, k_ref, v_ref, grad_ref, entries_ref, arrive_ref, sums_ref, turned_ref,
    gq_ref, gk_ref, gv_ref,
):
    length = q_ref.shape[0]
    blocks = length // BLOCK
    sums, turned = sums_ref[...], turned_ref[...]
    for b in range(blocks):
        at = b * BLOCK
        whole = slice(at, at + BLOCK)
        if b < blocks - 1:
            tail = jnp.exp(last_of(sums, b) - column(turned, at, BLOCK))
            later = arrive_ref[b]
            gk_ref[whole, :] = tail * exact_dot(v_ref[whole, :], later, 1, 1)
            gv_ref[whole, :] = tail * exact_dot(k_ref[whole, :], later)
        else:
            gk_ref[whole, :] = jnp.zeros((BLOCK, HEAD_DIM), f32)
            gv_ref[whole, :] = jnp.zeros((BLOCK, HEAD_DIM), f32)
        for i in range(BLOCK // TILE):
            rows = slice(at + i * TILE, at + (i + 1) * TILE)
            cols = slice(at, at + (i + 1) * TILE)
            table = weights_tile(sums, turned, at, i)
            q, g = q_ref[rows, :], grad_ref[rows, :]
            wq = (dot(q, k_ref[cols, :], 1, 1) * table).astype(bf16)
            gw = (dot(g, v_ref[cols, :], 1, 1) * table).astype(bf16)
            front = jnp.exp(column(turned, at + i * TILE, TILE))
            grad_q = dot(gw, k_ref[cols, :]) + front * exact_dot(g, entries_ref[b], 1, 1)
            gq_ref[rows, :] = grad_q.astype(bf16)
            gk_ref[cols, :] += dot(gw, q, 0, 0)
            gv_ref[cols, :] += dot(wq, g, 0, 0)


def finish_kernel(k_ref, v_ref, gk_ref, gv_ref, state_ref, sums_ref, turned_ref, ok_ref, ov_ref):
    length = k_ref.shape[0]
    blocks = length // BLOCK
    sums, turned = sums_ref[...], turned_ref[...]
    after = jnp.zeros((1, 1), f32)
    for b in reversed(range(blocks)):
        at = b * BLOCK
        rows = slice(at, at + BLOCK)
        tail = jnp.exp(last_of(sums, b) - column(turned, at, BLOCK))
        state = state_ref[...] * jnp.exp(after) if b < blocks - 1 else state_ref[...]
        after = after + last_of(sums, b)
        ok_ref[rows, :] = (gk_ref[rows, :] + tail * exact_dot(v_ref[rows, :], state, 1, 1)).astype(bf16)
        ov_ref[rows, :] = (gv_ref[rows, :] + tail * exact_dot(k_ref[rows, :], state)).astype(bf16)


def call(kernel, name, out, *args, cost=2e6):
    shapes = [jax.ShapeDtypeStruct(s, d) for s, d in out]
    return pl.pallas_call(
        kernel,
        out_shape=shapes,
        in_specs=[pl.BlockSpec(memory_space=pltpu.VMEM)] * len(args),
        out_specs=[pl.BlockSpec(memory_space=pltpu.VMEM)] * len(out),
        compiler_params=pltpu.CompilerParams(vmem_limit_bytes=32 << 20),
        cost_estimate=pl.CostEstimate(flops=int(cost), bytes_accessed=int(cost), transcendentals=0),
        name=name,
    )(*args)


def exchange(x, axis):
    return lax.all_to_all(x, axis, 0, 0)


def on_device(queries, key_rows, value_rows, gate_input, norm_gain, log_decay, grad_output):
    length = queries.shape[0]
    n_ctx, n_exp, n_section = (lax.axis_size(a) for a in ("ctx", "exp", "section"))
    width = HEAD_DIM * n_exp * n_section
    blocks = length // BLOCK
    chunks = length // CHUNK
    part = HEAD_DIM // n_ctx
    rates = log_decay.reshape(chunks, CHUNK)
    gain = norm_gain.reshape(1, HEAD_DIM)
    full, half = ((length, HEAD_DIM), f32), ((length, HEAD_DIM), bf16)
    states = ((blocks, HEAD_DIM, HEAD_DIM), f32)
    inner = ((max(blocks - 1, 1), HEAD_DIM, HEAD_DIM), f32)

    sent, entry, sums, turned = call(
        partial(states_kernel, n_ctx), "states",
        [((n_ctx, 2 * part, HEAD_DIM), f32), inner, ((chunks, CHUNK), f32), ((CHUNK, chunks), f32)],
        key_rows, value_rows, rates,
    )
    got = exchange(sent, "ctx")
    (local,) = call(local_kernel, "local", [full], queries, key_rows, value_rows, sums, turned)
    prefix, totals = call(
        partial(prefix_kernel, n_ctx), "prefix",
        [((n_ctx, part, HEAD_DIM), f32)] * 2, got,
    )
    state = exchange(prefix, "ctx").reshape(HEAD_DIM, HEAD_DIM)
    prob, signal = call(gate_kernel, "gate", [full, full], gate_input, grad_output, gain)
    attn, entries, sent = call(
        partial(attn_kernel, n_exp), "attn", [full, states, ((n_exp, 16, CHUNK), f32)],
        queries, local, state, entry, sums, turned, signal,
    )
    got = exchange(sent, "exp")
    (sent,) = call(
        partial(relay_kernel, n_exp, n_section), "relay", [((n_section, 16, CHUNK), f32)], got
    )
    got = exchange(sent, "section")
    grad, sent, arrive, inverse = call(
        partial(grad_kernel, n_section, width, n_ctx), "grad",
        [half, ((n_ctx, part, HEAD_DIM), f32), inner, ((CHUNK, 2 * chunks), f32)],
        got, attn, signal, queries, sums, turned,
    )
    got = exchange(sent, "ctx")
    grad_q, local_k, local_v = call(
        backward_kernel, "backward", [half, full, full],
        queries, key_rows, value_rows, grad, entries, arrive, sums, turned,
    )
    (suffix,) = call(
        partial(suffix_kernel, n_ctx), "suffix", [((n_ctx, part, HEAD_DIM), f32)], got, totals
    )
    later = exchange(suffix, "ctx").reshape(HEAD_DIM, HEAD_DIM)
    layer_out, grad_gate = call(
        output_kernel, "output", [half, half], attn, inverse, prob, gain, grad_output
    )
    grad_k, grad_v = call(
        finish_kernel, "finish", [half, half],
        key_rows, value_rows, local_k, local_v, later, sums, turned,
    )
    return layer_out, grad_q, grad_k, grad_v, grad_gate


def solution(mesh):
    block = P("ctx", ("section", "exp"))
    in_specs = (
        block, block, block, block, P(("section", "exp")), P(("section", "exp"), "ctx"), block,
    )
    return jax.shard_map(
        on_device, mesh=mesh, in_specs=in_specs, out_specs=(block,) * 5, check_vma=False
    )
```

time: 480 us -> 103 us (0.21)
  blocking collectives: 266 us -> 71.1 us
  waiting for transfers between devices: 121 us -> 9.53 us
  other arithmetic: 28.5 us -> 0 us
  local copies, waits for them, and re-layouts: 29.5 us -> 3.96 us
  between operations: 14.3 us -> 0.78 us
  matrix products: 12.7 us -> 0 us
  Pallas kernels: 0 us -> 10.5 us
  starting transfers between devices: 0.08 us -> 6.83 us
  loops' own time: 6.11 us -> 0 us
    psum x2 -> x0, blocking collectives: 229 us -> none  [the longest x1 118 us: on_device(): squares = lax.psum(jnp.sum(full_out * full_out, axis=1), ('section', 'exp'))]
    all_gather x2 -> x0, waiting for transfers between devices: 121 us -> none  [entering_2(): gathered = jax.tree.map(lambda a: lax.all_gather(a, axis), part)]
    all_to_all x0 -> x4, blocking collectives: none -> 71.1 us  [exchange(): return lax.all_to_all(x, axis, 0, 0)]
    unnamed x1 -> x0, blocking collectives: 37.1 us -> none
    add x15 -> x0, other arithmetic: 22.6 us -> none  [the longest x14 21.1 us: join_backward(): later_part[0] + jnp.exp(later_part[1])[:, None, None] * earlier[0]]
    dot_general x26 -> x0, matrix products: 12.7 us -> none  [the longest x2 2.27 us: block_backward(): jnp.dot(grad_float, entering.T, precision=precise)]
    pallas_call x0 -> x11, Pallas kernels: none -> 10.5 us  [call(): pl.pallas_call(kernel, out_shape=shapes, in_specs=[pl.BlockSpec(memory_sp...]
    unnamed x42 -> x26, local copies, waits for them, and re-layouts: 13.7 us -> 3.96 us
  transfers between devices with their start and end apart: 2 -> 2, of which waited for: 2 -> 2; matrix products, arithmetic and copies ran while one was open for 2% -> 0% of each run, Pallas kernels for 0% -> 5%
where the time goes in v1:
time: 103 us
  blocking collectives  71.1 us (69%)
  Pallas kernels  10.5 us (10%)
  waiting for transfers between devices  9.53 us (9%)
  starting transfers between devices  6.83 us (7%)
  local copies, waits for them, and re-layouts  3.96 us (4%)
    all_to_all x4, blocking collectives, exchange(): return lax.all_to_all(x, axis, 0, 0)  71.1 us
    pallas_call x11, Pallas kernels, call(): pl.pallas_call(kernel, out_shape=shapes, in_specs=[pl.BlockSpec(memory_sp...  10.5 us
    all_to_all x2, waiting for transfers between devices, exchange(): return lax.all_to_all(x, axis, 0, 0)  9.53 us
    all_to_all x2, starting transfers between devices, exchange(): return lax.all_to_all(x, axis, 0, 0)  6.83 us
    unnamed x26, local copies, waits for them, and re-layouts  3.96 us
  transfers between devices with their start and end apart: 2, of which 2 were waited for; matrix products, arithmetic and copies ran while one was open for 0% of the time, Pallas kernels for 5%

profile of v1, /device:TPU:1, one launch (start us, length us, event | category | flops | bytes accessed | tf_op | source)
XLA Modules:
  0.0 102.6 jit_solution(17897263506558065250)
XLA Ops:
  0.6 0.9 copy-done
  1.6 0.9 copy-done.2
  2.5 0.7 copy-done.11
  3.2 1.0 %states.1 = (f32[16,16,128]{2,1,0:T(8,128)S(1)}, f32[1,128,128]{2,1,0:T(8,128)S(1)}, f32[8,128]{1,0:T(8,128)S(1)}, f32[128,8]{1,0:T(8,128)S(1)}) custom-call(bf16[1024,128]{1,0:T(8,128)(2,1)S(1)} %copy-done, bf16[1024,128]{1,0:T(8,128)(2,1)S(1)} %copy-done.2, f32[8,128]{1,0:T(8,128)S(1)} %bitcast.6), custom_call_target="tpu_custom_call" | custom-call | flops 2000000 | bytes 2000000 | tf_op jit(solution)/shard_map/states/pallas_call | solution.py:287
  4.3 25.8 %all_to_all.30.got_ref = f32[16,16,128]{2,1,0:T(8,128)S(1)} all-to-all(f32[16,16,128]{2,1,0:T(8,128)S(1)} %get-tuple-element.29), channel_id=1, replica_groups=mesh['section'=4,'ctx'=16,'exp'=16] {'ctx'}, dimensions={0} | all-to-all | bytes 262144 | tf_op jit(solution)/shard_map/all_to_all | solution.py:299
  30.1 0.7 prefix.1
  30.8 3.4 %all-to-all-start.1 = ((f32[16,8,128]{2,1,0:T(8,128)}), f32[16,8,128]{2,1,0:T(8,128)S(1)}, u32[]{:S(2)}, u32[]{:S(2)}) async-start(f32[16,8,128]{2,1,0:T(8,128)} %get-tuple-element.30), calls=%async_computation.1 | async-start | bytes 131072 | tf_op jit(solution)/shard_map/all_to_all | solution.py:299
  34.3 0.9 local.1.local_ref
  35.2 0.0 copy-done.6
  35.3 0.6 copy-done.12
  35.9 0.1 gate.1
  36.0 5.4 %all-to-all-done.1 = f32[16,8,128]{2,1,0:T(8,128)S(1)} async-done(((f32[16,8,128]{2,1,0:T(8,128)}), f32[16,8,128]{2,1,0:T(8,128)S(1)}, u32[]{:S(2)}, u32[]{:S(2)}) %all-to-all-start.1) | async-done | bytes 65568 | tf_op jit(solution)/shard_map/all_to_all | solution.py:299
  41.4 0.9 attn.1
  42.4 0.7 copy-done.7
  43.0 22.3 %all_to_all.31.got_ref = f32[16,16,128]{2,1,0:T(8,128)S(1)} all-to-all(f32[16,16,128]{2,1,0:T(8,128)S(1)} %get-tuple-element.34), channel_id=1, replica_groups=mesh['section'=4,'ctx'=16,'exp'=16] {'exp'}, dimensions={0} | all-to-all | bytes 262144 | tf_op jit(solution)/shard_map/all_to_all | solution.py:299
  65.4 8.1 %all_to_all.32.got_ref = f32[4,16,128]{2,1,0:T(8,128)S(1)} all-to-all(f32[4,16,128]{2,1,0:T(8,128)S(1)} %relay.1), channel_id=1, replica_groups=mesh['section'=4,'ctx'=16,'exp'=16] {'section'}, dimensions={0} | all-to-all | bytes 65536 | tf_op jit(solution)/shard_map/all_to_all | solution.py:299
  73.5 1.1 %grad.1 = (bf16[1024,128]{1,0:T(8,128)(2,1)S(1)}, f32[16,8,128]{2,1,0:T(8,128)S(1)}, f32[1,128,128]{2,1,0:T(8,128)S(1)}, f32[128,16]{1,0:T(8,128)S(1)}) custom-call(f32[4,16,128]{2,1,0:T(8,128)S(1)} %all_to_all.32.got_ref, f32[1024,128]{1,0:T(8,128)S(1)} %get-tuple-element.33.attn_ref, f32[1024,128]{1,0:T(8,128)S(1)} %get-tuple-element.32.signal_ref, ...), custom_call_target="tpu_custom_call" | custom-call | flops 2000000 | bytes 2000000 | tf_op jit(solution)/shard_map/grad/pallas_call | solution.py:287
  74.6 14.8 %all_to_all.33.got_ref = f32[16,8,128]{2,1,0:T(8,128)S(1)} all-to-all(f32[16,8,128]{2,1,0:T(8,128)S(1)} %get-tuple-element.44), channel_id=1, replica_groups=mesh['section'=4,'ctx'=16,'exp'=16] {'ctx'}, dimensions={0} | all-to-all | bytes 131072 | tf_op jit(solution)/shard_map/all_to_all | solution.py:299
  89.4 0.7 suffix.1
  90.0 3.4 %all-to-all-start.5 = ((f32[16,8,128]{2,1,0:T(8,128)}), f32[16,8,128]{2,1,0:T(8,128)S(1)}, u32[]{:S(2)}, u32[]{:S(2)}) async-start(f32[16,8,128]{2,1,0:T(8,128)} %suffix.1), calls=%async_computation.5 | async-start | bytes 131072 | tf_op jit(solution)/shard_map/all_to_all | solution.py:299
  93.5 1.1 %output.1 = (bf16[1024,128]{1,0:T(8,128)(2,1)}, bf16[1024,128]{1,0:T(8,128)(2,1)}) custom-call(f32[1024,128]{1,0:T(8,128)S(1)} %get-tuple-element.33.attn_ref, f32[128,16]{1,0:T(8,128)S(1)} %get-tuple-element.35.inverse_ref, f32[1024,128]{1,0:T(8,128)S(1)} %get-tuple-element.36.prob_ref, f32[1,128]{1,0:T(1,128)S(1)} %bitcast.8, bf16[1024,128]{1,0:T(8,128)(2,1)S(1)} %copy-done.5), custom_call_target="tpu_custom_call" | custom-call | flops 2000000 | bytes 2000000 | tf_op jit(solution)/shard_map/output/pallas_call | solution.py:287
  94.5 2.6 %backward.1 = (bf16[1024,128]{1,0:T(8,128)(2,1)}, f32[1024,128]{1,0:T(8,128)S(1)}, f32[1024,128]{1,0:T(8,128)S(1)}) custom-call(bf16[1024,128]{1,0:T(8,128)(2,1)S(1)} %copy-done.4, bf16[1024,128]{1,0:T(8,128)(2,1)S(1)} %copy-done.1, bf16[1024,128]{1,0:T(8,128)(2,1)S(1)} %copy-done.3, bf16[1024,128]{1,0:T(8,128)(2,1)S(1)} %get-tuple-element.38.grad_ref, ...), custom_call_target="tpu_custom_call" | custom-call | flops 2000000 | bytes 2000000 | tf_op jit(solution)/shard_map/backward/pallas_call | solution.py:287
  97.2 4.1 %all-to-all-done.5 = f32[16,8,128]{2,1,0:T(8,128)S(1)} async-done(((f32[16,8,128]{2,1,0:T(8,128)}), f32[16,8,128]{2,1,0:T(8,128)S(1)}, u32[]{:S(2)}, u32[]{:S(2)}) %all-to-all-start.5) | async-done | bytes 65568 | tf_op jit(solution)/shard_map/all_to_all | solution.py:299
  101.3 1.4 %finish.1 = (bf16[1024,128]{1,0:T(8,128)(2,1)}, bf16[1024,128]{1,0:T(8,128)(2,1)}) custom-call(bf16[1024,128]{1,0:T(8,128)(2,1)S(1)} %copy-done.1, bf16[1024,128]{1,0:T(8,128)(2,1)S(1)} %copy-done.3, f32[1024,128]{1,0:T(8,128)S(1)} %get-tuple-element.42.gk_ref, f32[1024,128]{1,0:T(8,128)S(1)} %get-tuple-element.43.gv_ref, f32[128,128]{1,0:T(8,128)S(1)} %bitcast.5, ...), custom_call_target="tpu_custom_call" | custom-call | flops 2000000 | bytes 2000000 | tf_op jit(solution)/shard_map/finish/pallas_call | solution.py:287
  (21 shorter events, 0.1 us)
Async XLA Ops:
  0.6 1.0 copy-start
  1.6 0.9 copy-start.2
  2.5 0.7 copy-start.11
  3.2 31.0 %copy-start.4 = (bf16[1024,128]{1,0:T(8,128)(2,1)S(1)}, bf16[1024,128]{1,0:T(8,128)(2,1)}, u32[]{:S(2)}) copy-start(bf16[1024,128]{1,0:T(8,128)(2,1)} %q_ref.7) | copy-start | bytes 786436
  4.3 30.0 %copy-start.1 = (bf16[1024,128]{1,0:T(8,128)(2,1)S(1)}, bf16[1024,128]{1,0:T(8,128)(2,1)}, u32[]{:S(2)}) copy-start(bf16[1024,128]{1,0:T(8,128)(2,1)} %k_ref.7) | copy-start | bytes 786436
  4.3 29.9 %copy-start.3 = (bf16[1024,128]{1,0:T(8,128)(2,1)S(1)}, bf16[1024,128]{1,0:T(8,128)(2,1)}, u32[]{:S(2)}) copy-start(bf16[1024,128]{1,0:T(8,128)(2,1)} %v_ref.7) | copy-start | bytes 786436
  30.8 10.6 %all-to-all-start.1 = ((f32[16,8,128]{2,1,0:T(8,128)}), f32[16,8,128]{2,1,0:T(8,128)S(1)}, u32[]{:S(2)}, u32[]{:S(2)}) async-start(f32[16,8,128]{2,1,0:T(8,128)} %get-tuple-element.30), calls=%async_computation.1 | async-start | bytes 131072 | tf_op jit(solution)/shard_map/all_to_all | solution.py:299
  34.2 1.0 copy-start.5
  34.2 1.0 copy-start.6
  35.2 0.7 copy-start.12
  42.4 0.7 copy-start.7
  74.5 14.8 %copy-start.9 = (f32[1,128,128]{2,1,0:T(8,128)}, f32[1,128,128]{2,1,0:T(8,128)S(1)}, u32[]{:S(2)}) copy-start(f32[1,128,128]{2,1,0:T(8,128)S(1)} %get-tuple-element.40.arrive_ref) | copy-start | bytes 196612
  90.0 11.3 %all-to-all-start.5 = ((f32[16,8,128]{2,1,0:T(8,128)}), f32[16,8,128]{2,1,0:T(8,128)S(1)}, u32[]{:S(2)}, u32[]{:S(2)}) async-start(f32[16,8,128]{2,1,0:T(8,128)} %suffix.1), calls=%async_computation.5 | async-start | bytes 131072 | tf_op jit(solution)/shard_map/all_to_all | solution.py:299
  93.5 1.1 %copy-start.8 = (f32[2,128,128]{2,1,0:T(8,128)S(1)}, f32[2,128,128]{2,1,0:T(8,128)}, u32[]{:S(2)}) copy-start(f32[2,128,128]{2,1,0:T(8,128)} %copy-done.7) | copy-start | bytes 393220
  93.5 1.1 %copy-start.10 = (f32[1,128,128]{2,1,0:T(8,128)S(1)}, f32[1,128,128]{2,1,0:T(8,128)}, u32[]{:S(2)}) copy-start(f32[1,128,128]{2,1,0:T(8,128)} %copy-done.9) | copy-start | bytes 196612

commit v2 on v1

v2 whole, which is shorter than its diff:
```python
from functools import partial

import jax
import jax.numpy as jnp
from jax import lax
from jax.experimental import pallas as pl
from jax.experimental.pallas import tpu as pltpu
from jax.sharding import PartitionSpec as P

HEAD_DIM = 128
BLOCK = 512
TILE = 256
CHUNK = 128
EPSILON = 1e-06
f32 = jnp.float32
bf16 = jnp.bfloat16


def dot(a, b, ca=1, cb=0):
    return lax.dot_general(a, b, (((ca,), (cb,)), ((), ())), preferred_element_type=f32)


def split3(x):
    hi = x.astype(bf16)
    rest = x - hi.astype(f32)
    mid = rest.astype(bf16)
    return hi, mid, (rest - mid.astype(f32)).astype(bf16)


def exact_dot(a, b, turned=False):
    hi, mid, lo = split3(b)
    twice = jnp.concatenate([a, a], axis=1)
    zero = jnp.zeros_like(hi)
    if turned:
        left = jnp.concatenate([hi, mid], axis=1)
        right = jnp.concatenate([lo, zero], axis=1)
        both = dot(twice, jnp.concatenate([left, right], axis=0), 1, 1)
    else:
        left = jnp.concatenate([hi, mid], axis=0)
        right = jnp.concatenate([lo, zero], axis=0)
        both = dot(twice, jnp.concatenate([left, right], axis=1))
    half = both.shape[1] // 2
    return both[:, :half] + both[:, half:]


def exact_outer(a, b):
    parts = dot(a, jnp.concatenate(split3(b), axis=1), 0, 0)
    width = b.shape[1]
    return parts[:, :width] + (parts[:, width : 2 * width] + parts[:, 2 * width :])


def cumulate(rates):
    rows = rates.shape[0]
    per_block = BLOCK // CHUNK
    r = lax.broadcasted_iota(jnp.int32, (CHUNK, CHUNK), 0)
    c = lax.broadcasted_iota(jnp.int32, (CHUNK, CHUNK), 1)
    upper = jnp.where(r <= c, 1.0, 0.0).astype(bf16)
    hi, mid, lo = split3(rates)
    within = dot(hi, upper) + (dot(mid, upper) + dot(lo, upper))
    total = within[:, CHUNK - 1 :]
    pieces = []
    for row in range(rows):
        value = within[row : row + 1, :]
        for earlier in range(row // per_block * per_block, row):
            value = value + total[earlier : earlier + 1, :]
        pieces.append(value)
    return jnp.concatenate(pieces, axis=0)


def column(turned, first, count):
    return jnp.concatenate(
        [turned[:, r : r + 1] for r in range(first // CHUNK, (first + count) // CHUNK)], axis=0
    )


def row_of(sums, first, count):
    return jnp.concatenate(
        [sums[r : r + 1, :] for r in range(first // CHUNK, (first + count) // CHUNK)], axis=1
    )


def last_of(sums, block):
    row = (block + 1) * BLOCK // CHUNK - 1
    return sums[row : row + 1, CHUNK - 1 :]


def weights_tile(sums, turned, start, tile):
    first = start + tile * TILE
    width = (tile + 1) * TILE
    gap = column(turned, first, TILE) - row_of(sums, start, width)
    lower = jnp.exp(jnp.minimum(gap, 0.0))
    t = lax.broadcasted_iota(jnp.int32, (TILE, width), 0) + tile * TILE
    s = lax.broadcasted_iota(jnp.int32, (TILE, width), 1)
    return jnp.where(t >= s, lower, 0.0)


def core_of():
    return lax.rem(lax.axis_index("ctx"), 2)


def states_kernel(
    k_hbm, v_hbm, rates_hbm, send_ref, keep_ref, entry_ref, sums_ref, turned_ref,
    k_ref, v_ref, rates_ref, state_ref, sems,
):
    length = k_ref.shape[0]
    blocks = length // BLOCK
    half = HEAD_DIM // 2
    copies = [pltpu.make_async_copy(rates_hbm, rates_ref, sems.at[0])]
    for b in range(blocks):
        rows = pl.ds(b * BLOCK, BLOCK)
        copies.append(pltpu.make_async_copy(v_hbm.at[rows], v_ref.at[rows], sems.at[2 * b + 1]))
        copies.append(pltpu.make_async_copy(k_hbm.at[rows], k_ref.at[rows], sems.at[2 * b + 2]))
    for copy in copies:
        copy.start()
    copies[0].wait()
    sums = cumulate(rates_ref[...])
    turned = sums.T
    sums_ref[...] = sums
    turned_ref[...] = turned
    state = None
    total = jnp.zeros((1, 1), f32)
    for b in range(blocks):
        at = b * BLOCK
        last = last_of(sums, b)
        tail = jnp.exp(last - column(turned, at, BLOCK))
        copies[2 * b + 1].wait()
        copies[2 * b + 2].wait()
        scaled = v_ref[at : at + BLOCK, :].astype(f32) * tail
        update = exact_outer(k_ref[at : at + BLOCK, :], scaled)
        state = update if state is None else jnp.exp(last) * state + update
        total = total + last
        if b < blocks - 1:
            entry_ref[b] = state
    state_ref[...] = state
    core = core_of()
    spread = jnp.broadcast_to(total, (8, HEAD_DIM))
    keep_ref[:half, :] = state_ref[pl.ds(pl.multiple_of(core * half, half), half), :]
    keep_ref[half:, :] = spread
    send_ref[:half, :] = state_ref[pl.ds(pl.multiple_of((1 - core) * half, half), half), :]
    send_ref[half:, :] = spread


def pair_kernel(n_chip, keep_ref, got_ref, send_ref, first_ref, totals_ref):
    half = HEAD_DIM // 2
    is_second = core_of() == 1
    mine, other = keep_ref[:half, :], got_ref[:half, :]
    mine_total, other_total = keep_ref[half:, :], got_ref[half:, :]
    first = jnp.where(is_second, other, mine)
    second = jnp.where(is_second, mine, other)
    second_total = jnp.where(is_second, mine_total, other_total)
    first_ref[...] = first
    totals_ref[:8, :] = jnp.where(is_second, other_total, mine_total)
    totals_ref[8:, :] = second_total
    chip = jnp.exp(second_total[:1, :]) * first + second
    for j in range(n_chip):
        send_ref[j, :half, :] = chip
        send_ref[j, half:, :] = mine_total + other_total


def prefix_kernel(n_chip, got_ref, first_ref, totals_ref, keep_ref, send_ref, chips_ref):
    half = HEAD_DIM // 2
    chip = lax.div(lax.axis_index("ctx"), 2)
    is_second = core_of() == 1
    state = jnp.zeros((half, HEAD_DIM), f32)
    for j in range(n_chip):
        total = got_ref[j, half : half + 1, :]
        chips_ref[j : j + 1, :] = total
        state = jnp.where(j < chip, jnp.exp(total) * state + got_ref[j, :half, :], state)
    after = jnp.exp(totals_ref[:1, :]) * state + first_ref[...]
    keep_ref[...] = jnp.where(is_second, after, state)
    send_ref[...] = jnp.where(is_second, state, after)


def back_pair_kernel(n_chip, keep_ref, got_ref, totals_ref, send_ref, second_ref):
    is_second = core_of() == 1
    mine, other = keep_ref[...], got_ref[...]
    first = jnp.where(is_second, other, mine)
    second = jnp.where(is_second, mine, other)
    second_ref[...] = second
    chip = jnp.exp(totals_ref[:1, :]) * second + first
    for j in range(n_chip):
        send_ref[j] = chip


def suffix_kernel(
    n_chip, got_ref, second_ref, totals_ref, chips_ref, after_ref, keep_ref, send_ref,
):
    del after_ref
    half = HEAD_DIM // 2
    chip = lax.div(lax.axis_index("ctx"), 2)
    is_second = core_of() == 1
    state = jnp.zeros((half, HEAD_DIM), f32)
    for j in reversed(range(n_chip)):
        total = chips_ref[j : j + 1, :]
        state = jnp.where(j > chip, jnp.exp(total) * state + got_ref[j], state)
    before = jnp.exp(totals_ref[8:9, :]) * state + second_ref[...]
    keep_ref[...] = jnp.where(is_second, state, before)
    send_ref[...] = jnp.where(is_second, before, state)


def whole_state(keep_ref, got_ref):
    is_second = core_of() == 1
    keep, got = keep_ref[...], got_ref[...]
    return jnp.concatenate(
        [jnp.where(is_second, got, keep), jnp.where(is_second, keep, got)], axis=0
    )


def local_kernel(q_ref, k_ref, v_ref, sums_ref, turned_ref, out_ref):
    length = q_ref.shape[0]
    sums, turned = sums_ref[...], turned_ref[...]
    for b in range(length // BLOCK):
        at = b * BLOCK
        for i in range(BLOCK // TILE):
            rows = slice(at + i * TILE, at + (i + 1) * TILE)
            cols = slice(at, at + (i + 1) * TILE)
            scores = dot(q_ref[rows, :], k_ref[cols, :], 1, 1)
            weights = (scores * weights_tile(sums, turned, at, i)).astype(bf16)
            out_ref[rows, :] = dot(weights, v_ref[cols, :])


def gate_kernel(gate_ref, grad_ref, gain_ref, signal_ref):
    prob = jax.nn.sigmoid(gate_ref[...].astype(f32))
    signal_ref[...] = grad_ref[...].astype(f32) * prob * gain_ref[...]


def row_sums(x):
    ones = jnp.ones((8, HEAD_DIM), bf16)
    flat = exact_dot(ones, x, True)
    rows = x.shape[0] // CHUNK
    at = lax.broadcasted_iota(jnp.int32, (rows, CHUNK), 0)
    out = flat[:, :CHUNK]
    for r in range(1, rows):
        out = jnp.where(at == r, flat[:, r * CHUNK : (r + 1) * CHUNK], out)
    return out


def attn_kernel(
    n_section, q_ref, local_ref, keep_ref, got_ref, entry_ref, sums_ref, turned_ref, signal_ref,
    attn_ref, send_ref,
):
    length = q_ref.shape[0]
    sums, turned = sums_ref[...], turned_ref[...]
    start = whole_state(keep_ref, got_ref)
    state, gone = start, jnp.zeros((1, 1), f32)
    for b in range(length // BLOCK):
        at = b * BLOCK
        rows = slice(at, at + BLOCK)
        if b:
            state = entry_ref[b - 1] + jnp.exp(gone) * start
        attn_ref[length + b * HEAD_DIM : length + (b + 1) * HEAD_DIM, :] = state
        front = jnp.exp(column(turned, at, BLOCK))
        attn_ref[rows, :] = local_ref[rows, :] + front * exact_dot(q_ref[rows, :], state)
        gone = gone + last_of(sums, b)
    attn = attn_ref[:length, :]
    squares = row_sums(attn * attn)
    dots = row_sums(signal_ref[...] * attn)
    for j in range(n_section):
        send_ref[j, :8, :] = squares
        send_ref[j, 8:, :] = dots


def relay_kernel(n_section, n_exp, got_ref, send_ref):
    total = got_ref[0]
    for j in range(1, n_section):
        total = total + got_ref[j]
    for j in range(n_exp):
        send_ref[j] = total


def grad_kernel(
    n_exp, width, got_ref, attn_ref, signal_ref, q_ref, sums_ref, turned_ref,
    grad_ref, keep_ref, send_ref, aux_ref, state_ref,
):
    length = q_ref.shape[0]
    half = HEAD_DIM // 2
    blocks = length // BLOCK
    sums, turned = sums_ref[...], turned_ref[...]
    total = got_ref[0]
    for j in range(1, n_exp):
        total = total + got_ref[j]
    inverse = lax.rsqrt(total[:8] / width + EPSILON)
    along = inverse * total[8:] / width
    both = jnp.concatenate([inverse, along], axis=0).T
    aux_ref[(blocks - 1) * HEAD_DIM :, :16] = both
    state = None
    for b in reversed(range(blocks)):
        at = b * BLOCK
        rows = slice(at, at + BLOCK)
        inv = column(both[:, :8], at, BLOCK)
        alo = column(both[:, 8:], at, BLOCK)
        normed = attn_ref[rows, :] * inv
        grad = (inv * (signal_ref[rows, :] - normed * alo)).astype(bf16)
        grad_ref[rows, :] = grad
        front = jnp.exp(column(turned, at, BLOCK))
        update = exact_outer(q_ref[rows, :], grad.astype(f32) * front)
        state = update if state is None else jnp.exp(last_of(sums, b)) * state + update
        if b:
            aux_ref[(b - 1) * HEAD_DIM : b * HEAD_DIM, :] = state
    state_ref[...] = state
    core = core_of()
    keep_ref[...] = state_ref[pl.ds(pl.multiple_of(core * half, half), half), :]
    send_ref[...] = state_ref[pl.ds(pl.multiple_of((1 - core) * half, half), half), :]


def backward_kernel(
    q_ref, k_ref, v_ref, grad_ref, attn_ref, aux_ref, sums_ref, turned_ref, gin_ref, gain_ref, gout_ref,
    layer_hbm, gate_hbm, gq_hbm, gk_ref, gv_ref, layer_ref, gate_ref, gq_ref, sems,
):
    length = q_ref.shape[0]
    blocks = length // BLOCK
    sums, turned = sums_ref[...], turned_ref[...]
    both = aux_ref[(blocks - 1) * HEAD_DIM :, :16]
    copies = []

    def leave(ref, hbm, b, kind):
        part = pl.ds(b * BLOCK, BLOCK)
        copies.append(pltpu.make_async_copy(ref.at[part], hbm.at[part], sems.at[3 * b + kind]))
        copies[-1].start()

    for b in range(blocks):
        rows = slice(b * BLOCK, (b + 1) * BLOCK)
        scaled = attn_ref[rows, :] * column(both[:, :8], b * BLOCK, BLOCK) * gain_ref[...]
        prob = jax.nn.sigmoid(gin_ref[rows, :].astype(f32))
        layer = scaled * prob
        layer_ref[rows, :] = layer.astype(bf16)
        leave(layer_ref, layer_hbm, b, 0)
        gate_ref[rows, :] = (gout_ref[rows, :].astype(f32) * layer * (1.0 - prob)).astype(bf16)
        leave(gate_ref, gate_hbm, b, 1)
    for b in range(blocks):
        at = b * BLOCK
        whole = slice(at, at + BLOCK)
        if b < blocks - 1:
            tail = jnp.exp(last_of(sums, b) - column(turned, at, BLOCK))
            later = aux_ref[b * HEAD_DIM : (b + 1) * HEAD_DIM, :]
            gk_ref[whole, :] = tail * exact_dot(v_ref[whole, :], later, True)
            gv_ref[whole, :] = tail * exact_dot(k_ref[whole, :], later)
        else:
            gk_ref[whole, :] = jnp.zeros((BLOCK, HEAD_DIM), f32)
            gv_ref[whole, :] = jnp.zeros((BLOCK, HEAD_DIM), f32)
        entering = attn_ref[length + b * HEAD_DIM : length + (b + 1) * HEAD_DIM, :]
        for i in range(BLOCK // TILE):
            rows = slice(at + i * TILE, at + (i + 1) * TILE)
            cols = slice(at, at + (i + 1) * TILE)
            table = weights_tile(sums, turned, at, i)
            q, g = q_ref[rows, :], grad_ref[rows, :]
            wq = (dot(q, k_ref[cols, :], 1, 1) * table).astype(bf16)
            gw = (dot(g, v_ref[cols, :], 1, 1) * table).astype(bf16)
            front = jnp.exp(column(turned, at + i * TILE, TILE))
            grad_q = dot(gw, k_ref[cols, :]) + front * exact_dot(g, entering, True)
            gq_ref[rows, :] = grad_q.astype(bf16)
            gk_ref[cols, :] += dot(gw, q, 0, 0)
            gv_ref[cols, :] += dot(wq, g, 0, 0)
        leave(gq_ref, gq_hbm, b, 2)
    for copy in copies:
        copy.wait()


def finish_kernel(
    k_ref, v_ref, gk_ref, gv_ref, keep_ref, got_ref, sums_ref, turned_ref, ok_hbm, ov_hbm,
    ok_ref, ov_ref, sems,
):
    length = k_ref.shape[0]
    blocks = length // BLOCK
    sums, turned = sums_ref[...], turned_ref[...]
    start = whole_state(keep_ref, got_ref)
    after = jnp.zeros((1, 1), f32)
    copies = []
    for b in reversed(range(blocks)):
        at = b * BLOCK
        rows = slice(at, at + BLOCK)
        tail = jnp.exp(last_of(sums, b) - column(turned, at, BLOCK))
        state = start * jnp.exp(after)
        after = after + last_of(sums, b)
        part = pl.ds(at, BLOCK)
        ok_ref[rows, :] = (gk_ref[rows, :] + tail * exact_dot(v_ref[rows, :], state, True)).astype(bf16)
        copies.append(pltpu.make_async_copy(ok_ref.at[part], ok_hbm.at[part], sems.at[2 * b]))
        copies[-1].start()
        ov_ref[rows, :] = (gv_ref[rows, :] + tail * exact_dot(k_ref[rows, :], state)).astype(bf16)
        copies.append(pltpu.make_async_copy(ov_ref.at[part], ov_hbm.at[part], sems.at[2 * b + 1]))
        copies[-1].start()
    for copy in copies:
        copy.wait()


def call(kernel, name, out, *args, cost=2e6, hbm_in=False, hbm_last=False, hbm_out=0, scratch=()):
    shapes = [jax.ShapeDtypeStruct(s, d) for s, d in out]
    places = [pltpu.HBM if hbm_in else pltpu.VMEM] * len(args)
    if hbm_last:
        places[-1] = pl.ANY
    place_out = [pltpu.HBM] * hbm_out + [pltpu.VMEM] * (len(out) - hbm_out)
    return pl.pallas_call(
        kernel,
        out_shape=shapes,
        in_specs=[pl.BlockSpec(memory_space=place) for place in places],
        out_specs=[pl.BlockSpec(memory_space=place) for place in place_out],
        scratch_shapes=scratch,
        compiler_params=pltpu.CompilerParams(vmem_limit_bytes=16 << 20),
        cost_estimate=pl.CostEstimate(flops=int(cost), bytes_accessed=int(cost), transcendentals=0),
        name=name,
    )(*args)


def exchange(x, axis, groups=None):
    return lax.all_to_all(x, axis, 0, 0, axis_index_groups=groups)


def on_device(queries, key_rows, value_rows, gate_input, norm_gain, log_decay, grad_output):
    length = queries.shape[0]
    n_ctx, n_exp, n_section = (lax.axis_size(a) for a in ("ctx", "exp", "section"))
    n_chip = n_ctx // 2
    width = HEAD_DIM * n_exp * n_section
    blocks = length // BLOCK
    chunks = length // CHUNK
    part = HEAD_DIM // 2
    pairs = [(i, i ^ 1) for i in range(n_ctx)]
    lines = [[2 * i + core for i in range(n_chip)] for core in range(2)]
    rates = log_decay.reshape(chunks, CHUNK)
    gain = norm_gain.reshape(1, HEAD_DIM)
    full, half = ((length, HEAD_DIM), f32), ((length, HEAD_DIM), bf16)
    piece, marked = ((part, HEAD_DIM), f32), ((part + 8, HEAD_DIM), f32)

    sent, keep, entry, sums, turned = call(
        states_kernel, "states",
        [marked, marked, ((blocks - 1, HEAD_DIM, HEAD_DIM), f32), ((chunks, CHUNK), f32),
         ((CHUNK, chunks), f32)],
        *(pltpu.with_memory_space_constraint(a, pltpu.HBM) for a in (key_rows, value_rows, rates)),
        hbm_in=True,
        scratch=[
            pltpu.VMEM((length, HEAD_DIM), bf16), pltpu.VMEM((length, HEAD_DIM), bf16),
            pltpu.VMEM((chunks, CHUNK), f32), pltpu.VMEM((HEAD_DIM, HEAD_DIM), f32),
            pltpu.SemaphoreType.DMA((2 * blocks + 1,)),
        ],
    )
    got = lax.ppermute(sent, "ctx", pairs)
    sent, first, totals = call(
        partial(pair_kernel, n_chip), "pair",
        [((n_chip, part + 8, HEAD_DIM), f32), piece, ((16, HEAD_DIM), f32)], keep, got,
    )
    got = exchange(sent, "ctx", lines)
    (local,) = call(local_kernel, "local", [full], queries, key_rows, value_rows, sums, turned)
    (signal,) = call(gate_kernel, "gate", [full], gate_input, grad_output, gain)
    keep, sent, chips = call(
        partial(prefix_kernel, n_chip), "prefix", [piece, piece, ((n_chip, HEAD_DIM), f32)],
        got, first, totals,
    )
    got = lax.ppermute(sent, "ctx", pairs)
    attn, sent = call(
        partial(attn_kernel, n_section), "attn",
        [((length + blocks * HEAD_DIM, HEAD_DIM), f32), ((n_section, 16, CHUNK), f32)],
        queries, local, keep, got, entry, sums, turned, signal,
    )
    got = exchange(sent, "section")
    (sent,) = call(
        partial(relay_kernel, n_section, n_exp), "relay", [((n_exp, 16, CHUNK), f32)], got
    )
    got = exchange(sent, "exp")
    grad, keep, sent, aux = call(
        partial(grad_kernel, n_exp, width), "grad",
        [half, piece, piece, ((blocks * HEAD_DIM, HEAD_DIM), f32)],
        got, attn, signal, queries, sums, turned,
        scratch=[pltpu.VMEM((HEAD_DIM, HEAD_DIM), f32)],
    )
    got = lax.ppermute(sent, "ctx", pairs)
    sent, second = call(
        partial(back_pair_kernel, n_chip), "back_pair",
        [((n_chip, part, HEAD_DIM), f32), piece], keep, got, totals,
    )
    got = exchange(sent, "ctx", lines)
    layer_out, grad_gate, grad_q, local_k, local_v = call(
        backward_kernel, "backward", [half, half, half, full, full],
        queries, key_rows, value_rows, grad, attn, aux, sums, turned, gate_input, gain, grad_output,
        hbm_out=3, scratch=[
            pltpu.VMEM((length, HEAD_DIM), bf16), pltpu.VMEM((length, HEAD_DIM), bf16),
            pltpu.VMEM((length, HEAD_DIM), bf16), pltpu.SemaphoreType.DMA((3 * blocks,)),
        ],
    )
    keep, sent = call(
        partial(suffix_kernel, n_chip), "suffix", [piece, piece], got, second, totals, chips, local_k, hbm_last=True,
    )
    got = lax.ppermute(sent, "ctx", pairs)
    grad_k, grad_v = call(
        finish_kernel, "finish", [half, half],
        key_rows, value_rows, local_k, local_v, keep, got, sums, turned, hbm_out=2,
        scratch=[
            pltpu.VMEM((length, HEAD_DIM), bf16), pltpu.VMEM((length, HEAD_DIM), bf16),
            pltpu.SemaphoreType.DMA((2 * blocks,)),
        ],
    )
    return layer_out, grad_q, grad_k, grad_v, grad_gate


def solution(mesh):
    block = P("ctx", ("section", "exp"))
    in_specs = (
        block, block, block, block, P(("section", "exp")), P(("section", "exp"), "ctx"), block,
    )
    return jax.shard_map(
        on_device, mesh=mesh, in_specs=in_specs, out_specs=(block,) * 5, check_vma=False
    )
```

time: 103 us -> 99.5 us (0.966)
  blocking collectives: 71.1 us -> 45.3 us
  starting transfers between devices: 6.83 us -> 30.4 us
  local copies, waits for them, and re-layouts: 3.96 us -> 1.63 us
  waiting for transfers between devices: 9.53 us -> 11.2 us
    ppermute x0 -> x4, starting transfers between devices: none -> 27 us  [on_device(): got = lax.ppermute(sent, 'ctx', pairs)]
    all_to_all x4 -> x3, blocking collectives: 71.1 us -> 45.3 us  [exchange(): return lax.all_to_all(x, axis, 0, 0, axis_index_groups=groups)]
    all_to_all x2 -> x1, starting transfers between devices: 6.83 us -> 3.41 us  [exchange(): return lax.all_to_all(x, axis, 0, 0, axis_index_groups=groups)]
    ppermute x0 -> x4, waiting for transfers between devices: none -> 2.52 us  [on_device(): got = lax.ppermute(sent, 'ctx', pairs)]
    unnamed x26 -> x16, local copies, waits for them, and re-layouts: 3.96 us -> 1.63 us
    all_to_all x2 -> x1, waiting for transfers between devices: 9.53 us -> 8.66 us  [exchange(): return lax.all_to_all(x, axis, 0, 0, axis_index_groups=groups)]
    pallas_call x11 -> x12, Pallas kernels: 10.5 us -> 9.7 us  [call(): pl.pallas_call(kernel, out_shape=shapes, in_specs=[pl.BlockSpec(memory_sp...]
  transfers between devices with their start and end apart: 2 -> 5, of which waited for: 2 -> 4; matrix products, arithmetic and copies ran while one was open for 0% -> 0% of each run, Pallas kernels for 5% -> 4%
where the time goes in v2:
time: 99.5 us; the launch traced here: 99 us
  blocking collectives  45.3 us (46%)
  starting transfers between devices  30.4 us (31%)
  waiting for transfers between devices  11.2 us (11%)
  Pallas kernels  9.7 us (10%)
  local copies, waits for them, and re-layouts  1.63 us (2%)
    all_to_all x3, blocking collectives, exchange(): return lax.all_to_all(x, axis, 0, 0, axis_index_groups=groups)  45.3 us
    ppermute x4, starting transfers between devices, on_device(): got = lax.ppermute(sent, 'ctx', pairs)  27 us
    pallas_call x12, Pallas kernels, call(): pl.pallas_call(kernel, out_shape=shapes, in_specs=[pl.BlockSpec(memory_sp...  9.7 us
    all_to_all x1, waiting for transfers between devices, exchange(): return lax.all_to_all(x, axis, 0, 0, axis_index_groups=groups)  8.66 us
    all_to_all x1, starting transfers between devices, exchange(): return lax.all_to_all(x, axis, 0, 0, axis_index_groups=groups)  3.41 us
    ppermute x4, waiting for transfers between devices, on_device(): got = lax.ppermute(sent, 'ctx', pairs)  2.52 us
  transfers between devices with their start and end apart: 5, of which 4 were waited for; matrix products, arithmetic and copies ran while one was open for 0% of the time, Pallas kernels for 4%

profile of v2, /device:TPU:1, one launch (start us, length us, event | category | flops | bytes accessed | tf_op | source)
XLA Modules:
  0.0 99.0 jit_solution(5632128813898999451)
XLA Ops:
  0.6 2.0 %states.1 = (f32[72,128]{1,0:T(8,128)S(1)}, f32[72,128]{1,0:T(8,128)S(1)}, f32[1,128,128]{2,1,0:T(8,128)S(1)}, f32[8,128]{1,0:T(8,128)S(1)}, f32[128,8]{1,0:T(8,128)S(1)}) custom-call(bf16[1024,128]{1,0:T(8,128)(2,1)} %k_ref.5, bf16[1024,128]{1,0:T(8,128)(2,1)} %v_ref.5, f32[8,128]{1,0:T(8,128)} %bitcast.4), custom_call_target="tpu_custom_call" | custom-call | flops 2000000 | bytes 2000000 | tf_op jit(solution)/shard_map/states/pallas_call | solution.py:392
  2.6 16.0 %collective-permute-start = (f32[72,128]{1,0:T(8,128)S(1)}, f32[72,128]{1,0:T(8,128)S(1)}, u32[]{:S(2)}, u32[]{:S(2)}) collective-permute-start(f32[72,128]{1,0:T(8,128)S(1)} %get-tuple-element.36), channel_id=1, source_target_pairs={{0,16},{16,0},{32,48},{48,32},{64,80},{80,64},{96,112},{112,96},{1... | collective-permute-start | bytes 110600 | tf_op jit(solution)/shard_map/ppermute | solution.py:435
  18.6 0.8 collective-permute-done.got_ref
  19.5 15.2 %all_to_all.20.got_ref = f32[8,72,128]{2,1,0:T(8,128)S(1)} all-to-all(f32[8,72,128]{2,1,0:T(8,128)S(1)} %get-tuple-element.37), channel_id=1, replica_groups={{0,32,64,96,128,160,192,224},{16,48,80,112,144,176,208,240},{1,33,65,97..., dimensions={0} | all-to-all | bytes 589824 | tf_op jit(solution)/shard_map/all_to_all | solution.py:405
  34.7 0.1 prefix.1
  34.8 2.9 %collective-permute-start.1 = (f32[64,128]{1,0:T(8,128)S(1)}, f32[64,128]{1,0:T(8,128)S(1)}, u32[]{:S(2)}, u32[]{:S(2)}) collective-permute-start(f32[64,128]{1,0:T(8,128)S(1)} %get-tuple-element.41), channel_id=1, source_target_pairs={{0,16},{16,0},{32,48},{48,32},{64,80},{80,64},{96,112},{112,96},{1... | collective-permute-start | bytes 98312 | tf_op jit(solution)/shard_map/ppermute | solution.py:447
  37.7 0.9 local.1.local_ref
  38.7 0.6 copy-done.7
  39.3 0.1 gate.1.signal_ref
  39.5 0.9 attn.1
  40.4 6.7 %all_to_all.21.got_ref = f32[4,16,128]{2,1,0:T(8,128)S(1)} all-to-all(f32[4,16,128]{2,1,0:T(8,128)S(1)} %get-tuple-element.43), channel_id=1, replica_groups=mesh['section'=4,'ctx'=16,'exp'=16] {'section'}, dimensions={0} | all-to-all | bytes 65536 | tf_op jit(solution)/shard_map/all_to_all | solution.py:405
  47.1 23.4 %all_to_all.22.got_ref = f32[16,16,128]{2,1,0:T(8,128)S(1)} all-to-all(f32[16,16,128]{2,1,0:T(8,128)S(1)} %relay.1), channel_id=1, replica_groups=mesh['section'=4,'ctx'=16,'exp'=16] {'exp'}, dimensions={0} | all-to-all | bytes 262144 | tf_op jit(solution)/shard_map/all_to_all | solution.py:405
  70.5 1.0 %grad.1 = (bf16[1024,128]{1,0:T(8,128)(2,1)S(1)}, f32[64,128]{1,0:T(8,128)S(1)}, f32[64,128]{1,0:T(8,128)S(1)}, f32[256,128]{1,0:T(8,128)S(1)}) custom-call(f32[16,16,128]{2,1,0:T(8,128)S(1)} %all_to_all.22.got_ref, f32[1280,128]{1,0:T(8,128)S(1)} %get-tuple-element.44.attn_ref, f32[1024,128]{1,0:T(8,128)S(1)} %gate.1.signal_ref, ...), custom_call_target="tpu_custom_call" | custom-call | flops 2000000 | bytes 2000000 | tf_op jit(solution)/shard_map/grad/pallas_call | solution.py:392
  71.6 5.6 %collective-permute-start.2 = (f32[64,128]{1,0:T(8,128)S(1)}, f32[64,128]{1,0:T(8,128)S(1)}, u32[]{:S(2)}, u32[]{:S(2)}) collective-permute-start(f32[64,128]{1,0:T(8,128)S(1)} %get-tuple-element.52), channel_id=1, source_target_pairs={{0,16},{16,0},{32,48},{48,32},{64,80},{80,64},{96,112},{112,96},{1... | collective-permute-start | bytes 98312 | tf_op jit(solution)/shard_map/ppermute | solution.py:464
  77.2 0.8 collective-permute-done.2.got_ref
  78.1 0.7 back_pair.1
  78.8 3.4 %all-to-all-start.3 = ((f32[8,64,128]{2,1,0:T(8,128)}), f32[8,64,128]{2,1,0:T(8,128)S(1)}, u32[]{:S(2)}, u32[]{:S(2)}) async-start(f32[8,64,128]{2,1,0:T(8,128)} %get-tuple-element.53), calls=%async_computation.3 | async-start | bytes 524288 | tf_op jit(solution)/shard_map/all_to_all | solution.py:405
  82.2 0.9 copy-done.6
  83.2 2.6 %backward.1 = (bf16[1024,128]{1,0:T(8,128)(2,1)}, bf16[1024,128]{1,0:T(8,128)(2,1)}, bf16[1024,128]{1,0:T(8,128)(2,1)}, f32[1024,128]{1,0:T(8,128)S(1)}, f32[1024,128]{1,0:T(8,128)S(1)}) custom-call(bf16[1024,128]{1,0:T(8,128)(2,1)S(1)} %copy-done, bf16[1024,128]{1,0:T(8,128)(2,1)S(1)} %copy-done.1, bf16[1024,128]{1,0:T(8,128)(2,1)S(1)} %copy-done.2, ...), custom_call_target="tpu_custom_call" | custom-call | flops 2000000 | bytes 2000000 | tf_op jit(solution)/shard_map/backward/pallas_call | solution.py:392
  85.8 8.7 %all-to-all-done.3.got_ref = f32[8,64,128]{2,1,0:T(8,128)S(1)} async-done(((f32[8,64,128]{2,1,0:T(8,128)}), f32[8,64,128]{2,1,0:T(8,128)S(1)}, u32[]{:S(2)}, u32[]{:S(2)}) %all-to-all-start.3) | async-done | bytes 262176 | tf_op jit(solution)/shard_map/all_to_all | solution.py:405
  94.5 0.1 suffix.1
  94.5 2.4 %collective-permute-start.3 = (f32[64,128]{1,0:T(8,128)S(1)}, f32[64,128]{1,0:T(8,128)S(1)}, u32[]{:S(2)}, u32[]{:S(2)}) collective-permute-start(f32[64,128]{1,0:T(8,128)S(1)} %get-tuple-element.57), channel_id=1, source_target_pairs={{0,16},{16,0},{32,48},{48,32},{64,80},{80,64},{96,112},{112,96},{1... | collective-permute-start | bytes 98312 | tf_op jit(solution)/shard_map/ppermute | solution.py:481
  96.9 0.8 collective-permute-done.3.got_ref
  97.8 1.2 %finish.1 = (bf16[1024,128]{1,0:T(8,128)(2,1)}, bf16[1024,128]{1,0:T(8,128)(2,1)}) custom-call(bf16[1024,128]{1,0:T(8,128)(2,1)S(1)} %copy-done.1, bf16[1024,128]{1,0:T(8,128)(2,1)S(1)} %copy-done.2, f32[1024,128]{1,0:T(8,128)S(1)} %get-tuple-element.49.after_ref.gk_ref, f32[1024,128]{1,0:T(8,128)S(1)} %get-tuple-element.50.gv_ref, ...), custom_call_target="tpu_custom_call" | custom-call | flops 2000000 | bytes 2000000 | tf_op jit(solution)/shard_map/finish/pallas_call | solution.py:392
  (17 shorter events, 0.1 us)
Async XLA Ops:
  2.6 16.9 %collective-permute-start = (f32[72,128]{1,0:T(8,128)S(1)}, f32[72,128]{1,0:T(8,128)S(1)}, u32[]{:S(2)}, u32[]{:S(2)}) collective-permute-start(f32[72,128]{1,0:T(8,128)S(1)} %get-tuple-element.36), channel_id=1, source_target_pairs={{0,16},{16,0},{32,48},{48,32},{64,80},{80,64},{96,112},{112,96},{1... | collective-permute-start | bytes 110600 | tf_op jit(solution)/shard_map/ppermute | solution.py:435
  19.5 18.2 %copy-start.1 = (bf16[1024,128]{1,0:T(8,128)(2,1)S(1)}, bf16[1024,128]{1,0:T(8,128)(2,1)}, u32[]{:S(2)}) copy-start(bf16[1024,128]{1,0:T(8,128)(2,1)} %k_ref.5) | copy-start | bytes 786436
  19.5 18.2 %copy-start.2 = (bf16[1024,128]{1,0:T(8,128)(2,1)S(1)}, bf16[1024,128]{1,0:T(8,128)(2,1)}, u32[]{:S(2)}) copy-start(bf16[1024,128]{1,0:T(8,128)(2,1)} %v_ref.5) | copy-start | bytes 786436
  34.7 3.0 %copy-start = (bf16[1024,128]{1,0:T(8,128)(2,1)S(1)}, bf16[1024,128]{1,0:T(8,128)(2,1)}, u32[]{:S(2)}) copy-start(bf16[1024,128]{1,0:T(8,128)(2,1)} %q_ref.7) | copy-start | bytes 786436
  34.8 4.7 %collective-permute-start.1 = (f32[64,128]{1,0:T(8,128)S(1)}, f32[64,128]{1,0:T(8,128)S(1)}, u32[]{:S(2)}, u32[]{:S(2)}) collective-permute-start(f32[64,128]{1,0:T(8,128)S(1)} %get-tuple-element.41), channel_id=1, source_target_pairs={{0,16},{16,0},{32,48},{48,32},{64,80},{80,64},{96,112},{112,96},{1... | collective-permute-start | bytes 98312 | tf_op jit(solution)/shard_map/ppermute | solution.py:447
  37.7 1.0 copy-start.3
  37.7 1.0 %copy-start.4 = (bf16[1024,128]{1,0:T(8,128)(2,1)S(1)}, bf16[1024,128]{1,0:T(8,128)(2,1)}, u32[]{:S(2)}) copy-start(bf16[1024,128]{1,0:T(8,128)(2,1)} %gout_ref.1) | copy-start | bytes 786436
  38.7 0.7 copy-start.7
  71.6 7.2 %copy-start.5 = (bf16[1024,128]{1,0:T(8,128)(2,1)}, bf16[1024,128]{1,0:T(8,128)(2,1)S(1)}, u32[]{:S(2)}) copy-start(bf16[1024,128]{1,0:T(8,128)(2,1)S(1)} %get-tuple-element.45.grad_ref) | copy-start | bytes 786436
  71.6 6.5 %collective-permute-start.2 = (f32[64,128]{1,0:T(8,128)S(1)}, f32[64,128]{1,0:T(8,128)S(1)}, u32[]{:S(2)}, u32[]{:S(2)}) collective-permute-start(f32[64,128]{1,0:T(8,128)S(1)} %get-tuple-element.52), channel_id=1, source_target_pairs={{0,16},{16,0},{32,48},{48,32},{64,80},{80,64},{96,112},{112,96},{1... | collective-permute-start | bytes 98312 | tf_op jit(solution)/shard_map/ppermute | solution.py:464
  78.8 15.7 %all-to-all-start.3 = ((f32[8,64,128]{2,1,0:T(8,128)}), f32[8,64,128]{2,1,0:T(8,128)S(1)}, u32[]{:S(2)}, u32[]{:S(2)}) async-start(f32[8,64,128]{2,1,0:T(8,128)} %get-tuple-element.53), calls=%async_computation.3 | async-start | bytes 524288 | tf_op jit(solution)/shard_map/all_to_all | solution.py:405
  82.2 1.0 copy-start.6
  94.5 3.2 %collective-permute-start.3 = (f32[64,128]{1,0:T(8,128)S(1)}, f32[64,128]{1,0:T(8,128)S(1)}, u32[]{:S(2)}, u32[]{:S(2)}) collective-permute-start(f32[64,128]{1,0:T(8,128)S(1)} %get-tuple-element.57), channel_id=1, source_target_pairs={{0,16},{16,0},{32,48},{48,32},{64,80},{80,64},{96,112},{112,96},{1... | collective-permute-start | bytes 98312 | tf_op jit(solution)/shard_map/ppermute | solution.py:481

commit v3 on v2

--- a/solution.py
+++ b/solution.py
@@ -67,9 +67,11 @@
     return jnp.concatenate(pieces, axis=0)
 
 
-def column(turned, first, count):
+def column(turned, first, count, kind=0):
+    skip = 8 * kind
     return jnp.concatenate(
-        [turned[:, r : r + 1] for r in range(first // CHUNK, (first + count) // CHUNK)], axis=0
+        [turned[:, skip + r : skip + r + 1] for r in range(first // CHUNK, (first + count) // CHUNK)],
+        axis=0,
     )
 
 
@@ -99,8 +101,8 @@
 
 
 def states_kernel(
-    k_hbm, v_hbm, rates_hbm, send_ref, keep_ref, entry_ref, sums_ref, turned_ref,
-    k_ref, v_ref, rates_ref, state_ref, sems,
+    k_hbm, v_hbm, rates_hbm, gain_hbm, send_ref, keep_ref, entry_ref, sums_ref, turned_ref, gain_ref, k_ref, v_ref,
+    rates_ref, state_ref, sems,
 ):
     length = k_ref.shape[0]
     blocks = length // BLOCK
@@ -110,11 +112,18 @@
         rows = pl.ds(b * BLOCK, BLOCK)
         copies.append(pltpu.make_async_copy(v_hbm.at[rows], v_ref.at[rows], sems.at[2 * b + 1]))
         copies.append(pltpu.make_async_copy(k_hbm.at[rows], k_ref.at[rows], sems.at[2 * b + 2]))
+    copies.append(pltpu.make_async_copy(gain_hbm, gain_ref, sems.at[2 * blocks + 1]))
     for copy in copies:
         copy.start()
     copies[0].wait()
     sums = cumulate(rates_ref[...])
-    turned = sums.T
+    row = lax.broadcasted_iota(jnp.int32, sums.shape, 0)
+    lasts = last_of(sums, 0)
+    for b in range(1, blocks):
+        lasts = jnp.where(row >= b * BLOCK // CHUNK, last_of(sums, b), lasts)
+    front = jnp.exp(sums)
+    tails = jnp.exp(lasts - sums)
+    turned = jnp.concatenate([sums, front, tails, jnp.zeros_like(sums)], axis=0).T
     sums_ref[...] = sums
     turned_ref[...] = turned
     state = None
@@ -122,7 +131,7 @@
     for b in range(blocks):
         at = b * BLOCK
         last = last_of(sums, b)
-        tail = jnp.exp(last - column(turned, at, BLOCK))
+        tail = column(turned, at, BLOCK, 2)
         copies[2 * b + 1].wait()
         copies[2 * b + 2].wait()
         scaled = v_ref[at : at + BLOCK, :].astype(f32) * tail
@@ -138,9 +147,11 @@
     keep_ref[half:, :] = spread
     send_ref[:half, :] = state_ref[pl.ds(pl.multiple_of((1 - core) * half, half), half), :]
     send_ref[half:, :] = spread
-
-
-def pair_kernel(n_chip, keep_ref, got_ref, send_ref, first_ref, totals_ref):
+    copies[-1].wait()
+
+
+def pair_kernel(n_chip, keep_ref, got_ref, after_ref, send_ref, first_ref, totals_ref):
+    del after_ref
     half = HEAD_DIM // 2
     is_second = core_of() == 1
     mine, other = keep_ref[:half, :], got_ref[:half, :]
@@ -171,7 +182,8 @@
     send_ref[...] = jnp.where(is_second, state, after)
 
 
-def back_pair_kernel(n_chip, keep_ref, got_ref, totals_ref, send_ref, second_ref):
+def back_pair_kernel(n_chip, keep_ref, got_ref, totals_ref, after_ref, send_ref, second_ref):
+    del after_ref
     is_second = core_of() == 1
     mine, other = keep_ref[...], got_ref[...]
     first = jnp.where(is_second, other, mine)
@@ -182,10 +194,7 @@
         send_ref[j] = chip
 
 
-def suffix_kernel(
-    n_chip, got_ref, second_ref, totals_ref, chips_ref, after_ref, keep_ref, send_ref,
-):
-    del after_ref
+def suffix_kernel(n_chip, got_ref, second_ref, totals_ref, chips_ref, keep_ref, send_ref):
     half = HEAD_DIM // 2
     chip = lax.div(lax.axis_index("ctx"), 2)
     is_second = core_of() == 1
@@ -225,14 +234,13 @@
 
 
 def row_sums(x):
-    ones = jnp.ones((8, HEAD_DIM), bf16)
-    flat = exact_dot(ones, x, True)
-    rows = x.shape[0] // CHUNK
-    at = lax.broadcasted_iota(jnp.int32, (rows, CHUNK), 0)
-    out = flat[:, :CHUNK]
-    for r in range(1, rows):
-        out = jnp.where(at == r, flat[:, r * CHUNK : (r + 1) * CHUNK], out)
-    return out
+    down = lax.broadcasted_iota(jnp.int32, (CHUNK, CHUNK), 0)
+    across = lax.broadcasted_iota(jnp.int32, (CHUNK, CHUNK), 1)
+    pieces = []
+    for r in range(x.shape[0] // CHUNK):
+        sums = jnp.sum(x[r * CHUNK : (r + 1) * CHUNK, :], axis=1, keepdims=True)
+        pieces.append(jnp.sum(jnp.where(down == across, sums, 0.0), axis=0, keepdims=True))
+    return jnp.concatenate(pieces, axis=0)
 
 
 def attn_kernel(
@@ -249,7 +257,7 @@
         if b:
             state = entry_ref[b - 1] + jnp.exp(gone) * start
         attn_ref[length + b * HEAD_DIM : length + (b + 1) * HEAD_DIM, :] = state
-        front = jnp.exp(column(turned, at, BLOCK))
+        front = column(turned, at, BLOCK, 1)
         attn_ref[rows, :] = local_ref[rows, :] + front * exact_dot(q_ref[rows, :], state)
         gone = gone + last_of(sums, b)
     attn = attn_ref[:length, :]
@@ -281,7 +289,7 @@
         total = total + got_ref[j]
     inverse = lax.rsqrt(total[:8] / width + EPSILON)
     along = inverse * total[8:] / width
-    both = jnp.concatenate([inverse, along], axis=0).T
+    both = jnp.concatenate([inverse, inverse * inverse * along], axis=0).T
     aux_ref[(blocks - 1) * HEAD_DIM :, :16] = both
     state = None
     for b in reversed(range(blocks)):
@@ -289,10 +297,9 @@
         rows = slice(at, at + BLOCK)
         inv = column(both[:, :8], at, BLOCK)
         alo = column(both[:, 8:], at, BLOCK)
-        normed = attn_ref[rows, :] * inv
-        grad = (inv * (signal_ref[rows, :] - normed * alo)).astype(bf16)
+        grad = (inv * signal_ref[rows, :] - alo * attn_ref[rows, :]).astype(bf16)
         grad_ref[rows, :] = grad
-        front = jnp.exp(column(turned, at, BLOCK))
+        front = column(turned, at, BLOCK, 1)
         update = exact_outer(q_ref[rows, :], grad.astype(f32) * front)
         state = update if state is None else jnp.exp(last_of(sums, b)) * state + update
         if b:
@@ -303,41 +310,42 @@
     send_ref[...] = state_ref[pl.ds(pl.multiple_of((1 - core) * half, half), half), :]
 
 
+def output_kernel(
+    attn_ref, aux_ref, gin_ref, gain_ref, gout_ref, layer_hbm, gate_hbm, done_ref, layer_ref, gate_ref, sems,
+):
+    length = gout_ref.shape[0]
+    done_ref[...] = jnp.zeros_like(done_ref)
+    both = aux_ref[aux_ref.shape[0] - HEAD_DIM :, :16]
+    copies = []
+    for b in range(length // BLOCK):
+        rows, part = slice(b * BLOCK, (b + 1) * BLOCK), pl.ds(b * BLOCK, BLOCK)
+        scaled = attn_ref[rows, :] * column(both, b * BLOCK, BLOCK) * gain_ref[...]
+        prob = jax.nn.sigmoid(gin_ref[rows, :].astype(f32))
+        layer = scaled * prob
+        layer_ref[rows, :] = layer.astype(bf16)
+        copies.append(pltpu.make_async_copy(layer_ref.at[part], layer_hbm.at[part], sems.at[2 * b]))
+        copies[-1].start()
+        gate_ref[rows, :] = (gout_ref[rows, :].astype(f32) * layer * (1.0 - prob)).astype(bf16)
+        copies.append(pltpu.make_async_copy(gate_ref.at[part], gate_hbm.at[part], sems.at[2 * b + 1]))
+        copies[-1].start()
+    for copy in copies:
+        copy.wait()
+
+
 def backward_kernel(
-    q_ref, k_ref, v_ref, grad_ref, attn_ref, aux_ref, sums_ref, turned_ref, gin_ref, gain_ref, gout_ref,
-    layer_hbm, gate_hbm, gq_hbm, gk_ref, gv_ref, layer_ref, gate_ref, gq_ref, sems,
+    q_ref, k_ref, v_ref, grad_ref, attn_ref, aux_ref, sums_ref, turned_ref,
+    gq_hbm, gk_ref, gv_ref, gq_ref, sems,
 ):
     length = q_ref.shape[0]
     blocks = length // BLOCK
     sums, turned = sums_ref[...], turned_ref[...]
-    both = aux_ref[(blocks - 1) * HEAD_DIM :, :16]
     copies = []
-
-    def leave(ref, hbm, b, kind):
-        part = pl.ds(b * BLOCK, BLOCK)
-        copies.append(pltpu.make_async_copy(ref.at[part], hbm.at[part], sems.at[3 * b + kind]))
-        copies[-1].start()
-
-    for b in range(blocks):
-        rows = slice(b * BLOCK, (b + 1) * BLOCK)
-        scaled = attn_ref[rows, :] * column(both[:, :8], b * BLOCK, BLOCK) * gain_ref[...]
-        prob = jax.nn.sigmoid(gin_ref[rows, :].astype(f32))
-        layer = scaled * prob
-        layer_ref[rows, :] = layer.astype(bf16)
-        leave(layer_ref, layer_hbm, b, 0)
-        gate_ref[rows, :] = (gout_ref[rows, :].astype(f32) * layer * (1.0 - prob)).astype(bf16)
-        leave(gate_ref, gate_hbm, b, 1)
     for b in range(blocks):
         at = b * BLOCK
         whole = slice(at, at + BLOCK)
+        later = None
         if b < blocks - 1:
-            tail = jnp.exp(last_of(sums, b) - column(turned, at, BLOCK))
             later = aux_ref[b * HEAD_DIM : (b + 1) * HEAD_DIM, :]
-            gk_ref[whole, :] = tail * exact_dot(v_ref[whole, :], later, True)
-            gv_ref[whole, :] = tail * exact_dot(k_ref[whole, :], later)
-        else:
-            gk_ref[whole, :] = jnp.zeros((BLOCK, HEAD_DIM), f32)
-            gv_ref[whole, :] = jnp.zeros((BLOCK, HEAD_DIM), f32)
         entering = attn_ref[length + b * HEAD_DIM : length + (b + 1) * HEAD_DIM, :]
         for i in range(BLOCK // TILE):
             rows = slice(at + i * TILE, at + (i + 1) * TILE)
@@ -346,12 +354,25 @@
             q, g = q_ref[rows, :], grad_ref[rows, :]
             wq = (dot(q, k_ref[cols, :], 1, 1) * table).astype(bf16)
             gw = (dot(g, v_ref[cols, :], 1, 1) * table).astype(bf16)
-            front = jnp.exp(column(turned, at + i * TILE, TILE))
+            front = column(turned, at + i * TILE, TILE, 1)
             grad_q = dot(gw, k_ref[cols, :]) + front * exact_dot(g, entering, True)
             gq_ref[rows, :] = grad_q.astype(bf16)
-            gk_ref[cols, :] += dot(gw, q, 0, 0)
-            gv_ref[cols, :] += dot(wq, g, 0, 0)
-        leave(gq_ref, gq_hbm, b, 2)
+            add_k, add_v = dot(gw, q, 0, 0), dot(wq, g, 0, 0)
+            if later is not None:
+                tail = column(turned, at + i * TILE, TILE, 2)
+                more_k = tail * exact_dot(v_ref[rows, :], later, True)
+                more_v = tail * exact_dot(k_ref[rows, :], later)
+            else:
+                more_k = more_v = 0.0
+            if i:
+                old = slice(at, at + i * TILE)
+                gk_ref[old, :] += add_k[: i * TILE, :]
+                gv_ref[old, :] += add_v[: i * TILE, :]
+            gk_ref[rows, :] = add_k[i * TILE :, :] + more_k
+            gv_ref[rows, :] = add_v[i * TILE :, :] + more_v
+        part = pl.ds(at, BLOCK)
+        copies.append(pltpu.make_async_copy(gq_ref.at[part], gq_hbm.at[part], sems.at[b]))
+        copies[-1].start()
     for copy in copies:
         copy.wait()
 
@@ -369,7 +390,7 @@
     for b in reversed(range(blocks)):
         at = b * BLOCK
         rows = slice(at, at + BLOCK)
-        tail = jnp.exp(last_of(sums, b) - column(turned, at, BLOCK))
+        tail = column(turned, at, BLOCK, 2)
         state = start * jnp.exp(after)
         after = after + last_of(sums, b)
         part = pl.ds(at, BLOCK)
@@ -416,29 +437,31 @@
     pairs = [(i, i ^ 1) for i in range(n_ctx)]
     lines = [[2 * i + core for i in range(n_chip)] for core in range(2)]
     rates = log_decay.reshape(chunks, CHUNK)
-    gain = norm_gain.reshape(1, HEAD_DIM)
     full, half = ((length, HEAD_DIM), f32), ((length, HEAD_DIM), bf16)
     piece, marked = ((part, HEAD_DIM), f32), ((part + 8, HEAD_DIM), f32)
 
-    sent, keep, entry, sums, turned = call(
+    sent, keep, entry, sums, turned, gain, held_k, held_v = call(
         states_kernel, "states",
         [marked, marked, ((blocks - 1, HEAD_DIM, HEAD_DIM), f32), ((chunks, CHUNK), f32),
-         ((CHUNK, chunks), f32)],
-        *(pltpu.with_memory_space_constraint(a, pltpu.HBM) for a in (key_rows, value_rows, rates)),
-        hbm_in=True,
+         ((CHUNK, 4 * chunks), f32), ((1, HEAD_DIM), f32), half, half],
+        *(
+            pltpu.with_memory_space_constraint(a, pltpu.HBM)
+            for a in (key_rows, value_rows, rates, norm_gain.reshape(1, HEAD_DIM))
+        ),
+        hbm_in=True, cost=1e7,
         scratch=[
-            pltpu.VMEM((length, HEAD_DIM), bf16), pltpu.VMEM((length, HEAD_DIM), bf16),
             pltpu.VMEM((chunks, CHUNK), f32), pltpu.VMEM((HEAD_DIM, HEAD_DIM), f32),
-            pltpu.SemaphoreType.DMA((2 * blocks + 1,)),
+            pltpu.SemaphoreType.DMA((2 * blocks + 2,)),
         ],
     )
     got = lax.ppermute(sent, "ctx", pairs)
+    (local,) = call(local_kernel, "local", [full], queries, held_k, held_v, sums, turned)
     sent, first, totals = call(
         partial(pair_kernel, n_chip), "pair",
-        [((n_chip, part + 8, HEAD_DIM), f32), piece, ((16, HEAD_DIM), f32)], keep, got,
+        [((n_chip, part + 8, HEAD_DIM), f32), piece, ((16, HEAD_DIM), f32)],
+        keep, got, local, hbm_last=True,
     )
     got = exchange(sent, "ctx", lines)
-    (local,) = call(local_kernel, "local", [full], queries, key_rows, value_rows, sums, turned)
     (signal,) = call(gate_kernel, "gate", [full], gate_input, grad_output, gain)
     keep, sent, chips = call(
         partial(prefix_kernel, n_chip), "prefix", [piece, piece, ((n_chip, HEAD_DIM), f32)],
@@ -462,31 +485,35 @@
         scratch=[pltpu.VMEM((HEAD_DIM, HEAD_DIM), f32)],
     )
     got = lax.ppermute(sent, "ctx", pairs)
-    sent, second = call(
-        partial(back_pair_kernel, n_chip), "back_pair",
-        [((n_chip, part, HEAD_DIM), f32), piece], keep, got, totals,
-    )
-    got = exchange(sent, "ctx", lines)
-    layer_out, grad_gate, grad_q, local_k, local_v = call(
-        backward_kernel, "backward", [half, half, half, full, full],
-        queries, key_rows, value_rows, grad, attn, aux, sums, turned, gate_input, gain, grad_output,
-        hbm_out=3, scratch=[
-            pltpu.VMEM((length, HEAD_DIM), bf16), pltpu.VMEM((length, HEAD_DIM), bf16),
-            pltpu.VMEM((length, HEAD_DIM), bf16), pltpu.SemaphoreType.DMA((3 * blocks,)),
-        ],
-    )
-    keep, sent = call(
-        partial(suffix_kernel, n_chip), "suffix", [piece, piece], got, second, totals, chips, local_k, hbm_last=True,
-    )
-    got = lax.ppermute(sent, "ctx", pairs)
-    grad_k, grad_v = call(
-        finish_kernel, "finish", [half, half],
-        key_rows, value_rows, local_k, local_v, keep, got, sums, turned, hbm_out=2,
+    layer_out, grad_gate, done = call(
+        output_kernel, "output", [half, half, ((8, HEAD_DIM), f32)], attn, aux, gate_input, gain, grad_output, hbm_out=2,
         scratch=[
             pltpu.VMEM((length, HEAD_DIM), bf16), pltpu.VMEM((length, HEAD_DIM), bf16),
             pltpu.SemaphoreType.DMA((2 * blocks,)),
         ],
     )
+    sent, second = call(
+        partial(back_pair_kernel, n_chip), "back_pair",
+        [((n_chip, part, HEAD_DIM), f32), piece], keep, got, totals, done,
+    )
+    got = exchange(sent, "ctx", lines)
+    grad_q, local_k, local_v = call(
+        backward_kernel, "backward", [half, full, full],
+        queries, held_k, held_v, grad, attn, aux, sums, turned, hbm_out=1,
+        scratch=[pltpu.VMEM((length, HEAD_DIM), bf16), pltpu.SemaphoreType.DMA((blocks,))],
+    )
+    keep, sent = call(
+        partial(suffix_kernel, n_chip), "suffix", [piece, piece], got, second, totals, chips
+    )
+    got = lax.ppermute(sent, "ctx", pairs)
+    grad_k, grad_v = call(
+        finish_kernel, "finish", [half, half],
+        held_k, held_v, local_k, local_v, keep, got, sums, turned, hbm_out=2,
+        scratch=[
+            pltpu.VMEM((length, HEAD_DIM), bf16), pltpu.VMEM((length, HEAD_DIM), bf16),
+            pltpu.SemaphoreType.DMA((2 * blocks,)),
+        ],
+    )
     return layer_out, grad_q, grad_k, grad_v, grad_gate
 
 

time: 99.5 us -> 98.8 us (level)
  blocking collectives: 45.3 us -> 60.1 us
  waiting for transfers between devices: 11.2 us -> 0.71 us
  starting transfers between devices: 30.4 us -> 27.2 us
  local copies, waits for them, and re-layouts: 1.63 us -> 0.01 us
    all_to_all x3 -> x4, blocking collectives: 45.3 us -> 60.1 us  [exchange(): return lax.all_to_all(x, axis, 0, 0, axis_index_groups=groups)]
    all_to_all x1 -> x0, waiting for transfers between devices: 8.66 us -> none  [exchange(): return lax.all_to_all(x, axis, 0, 0, axis_index_groups=groups)]
    all_to_all x1 -> x0, starting transfers between devices: 3.41 us -> none  [exchange(): return lax.all_to_all(x, axis, 0, 0, axis_index_groups=groups)]
    ppermute x4, waiting for transfers between devices: 2.52 us -> 0.71 us  [on_device(): got = lax.ppermute(sent, 'ctx', pairs)]
    unnamed x16 -> x6, local copies, waits for them, and re-layouts: 1.63 us -> 0.01 us
    pallas_call x12 -> x13, Pallas kernels: 9.7 us -> 9.67 us  [call(): pl.pallas_call(kernel, out_shape=shapes, in_specs=[pl.BlockSpec(memory_sp...]
  transfers between devices with their start and end apart: 5 -> 4, of which waited for: 4 -> 1; matrix products, arithmetic and copies ran while one was open for 0% -> 0% of each run, Pallas kernels for 4% -> 5%
where the time goes in v3:
time: 98.8 us; the launch traced here: 98.4 us
  blocking collectives  60.1 us (61%)
  starting transfers between devices  27.2 us (28%)
  Pallas kernels  9.67 us (10%)
    all_to_all x4, blocking collectives, exchange(): return lax.all_to_all(x, axis, 0, 0, axis_index_groups=groups)  60.1 us
    ppermute x4, starting transfers between devices, on_device(): got = lax.ppermute(sent, 'ctx', pairs)  27.2 us
    pallas_call x13, Pallas kernels, call(): pl.pallas_call(kernel, out_shape=shapes, in_specs=[pl.BlockSpec(memory_sp...  9.67 us
  transfers between devices with their start and end apart: 4, of which 1 were waited for; matrix products, arithmetic and copies ran while one was open for 0% of the time, Pallas kernels for 5%

profile of v3, /device:TPU:1, one launch (start us, length us, event | category | flops | bytes accessed | tf_op | source)
XLA Modules:
  0.0 98.4 jit_solution(4929498822073415671)
XLA Ops:
  0.6 0.0 copy-start
  0.6 2.0 %states.1 = (f32[72,128]{1,0:T(8,128)S(1)}, f32[72,128]{1,0:T(8,128)S(1)}, f32[1,128,128]{2,1,0:T(8,128)S(1)}, f32[8,128]{1,0:T(8,128)S(1)}, f32[128,32]{1,0:T(8...) custom-call(bf16[1024,128]{1,0:T(8,128)(2,1)} %k_hbm.1, ...), custom_call_target="tpu_custom_call" | custom-call | flops 10000000 | bytes 10000000 | tf_op jit(solution)/shard_map/states/pallas_call | solution.py:413
  2.7 16.0 %collective-permute-start = (f32[72,128]{1,0:T(8,128)S(1)}, f32[72,128]{1,0:T(8,128)S(1)}, u32[]{:S(2)}, u32[]{:S(2)}) collective-permute-start(f32[72,128]{1,0:T(8,128)S(1)} %get-tuple-element.42), channel_id=1, source_target_pairs={{0,16},{16,0},{32,48},{48,32},{64,80},{80,64},{96,112},{112,96},{1... | collective-permute-start | bytes 110600 | tf_op jit(solution)/shard_map/ppermute | solution.py:457
  18.7 0.9 local.1.after_ref.local_ref
  19.7 0.0 collective-permute-done.got_ref
  19.7 0.0 copy-start.2
  19.7 15.2 %all_to_all.20.got_ref = f32[8,72,128]{2,1,0:T(8,128)S(1)} all-to-all(f32[8,72,128]{2,1,0:T(8,128)S(1)} %get-tuple-element.43), channel_id=1, replica_groups={{0,32,64,96,128,160,192,224},{16,48,80,112,144,176,208,240},{1,33,65,97..., dimensions={0} | all-to-all | bytes 589824 | tf_op jit(solution)/shard_map/all_to_all | solution.py:426
  34.9 0.1 prefix.1
  35.0 2.9 %collective-permute-start.1 = (f32[64,128]{1,0:T(8,128)S(1)}, f32[64,128]{1,0:T(8,128)S(1)}, u32[]{:S(2)}, u32[]{:S(2)}) collective-permute-start(f32[64,128]{1,0:T(8,128)S(1)} %get-tuple-element.47), channel_id=1, source_target_pairs={{0,16},{16,0},{32,48},{48,32},{64,80},{80,64},{96,112},{112,96},{1... | collective-permute-start | bytes 98312 | tf_op jit(solution)/shard_map/ppermute | solution.py:470
  37.9 0.1 gate.1.signal_ref
  38.0 0.7 collective-permute-done.1.got_ref
  38.7 0.7 attn.1
  39.4 6.7 %all_to_all.21.got_ref = f32[4,16,128]{2,1,0:T(8,128)S(1)} all-to-all(f32[4,16,128]{2,1,0:T(8,128)S(1)} %get-tuple-element.51), channel_id=1, replica_groups=mesh['section'=4,'ctx'=16,'exp'=16] {'section'}, dimensions={0} | all-to-all | bytes 65536 | tf_op jit(solution)/shard_map/all_to_all | solution.py:426
  46.1 23.4 %all_to_all.22.got_ref = f32[16,16,128]{2,1,0:T(8,128)S(1)} all-to-all(f32[16,16,128]{2,1,0:T(8,128)S(1)} %relay.1), channel_id=1, replica_groups=mesh['section'=4,'ctx'=16,'exp'=16] {'exp'}, dimensions={0} | all-to-all | bytes 262144 | tf_op jit(solution)/shard_map/all_to_all | solution.py:426
  69.5 1.0 %grad.1 = (bf16[1024,128]{1,0:T(8,128)(2,1)S(1)}, f32[64,128]{1,0:T(8,128)S(1)}, f32[64,128]{1,0:T(8,128)S(1)}, f32[256,128]{1,0:T(8,128)S(1)}) custom-call(f32[16,16,128]{2,1,0:T(8,128)S(1)} %all_to_all.22.got_ref, f32[1280,128]{1,0:T(8,128)S(1)} %get-tuple-element.50.attn_ref, f32[1024,128]{1,0:T(8,128)S(1)} %gate.1.signal_ref, ...), custom_call_target="tpu_custom_call" | custom-call | flops 2000000 | bytes 2000000 | tf_op jit(solution)/shard_map/grad/pallas_call | solution.py:413
  70.5 5.9 %collective-permute-start.2 = (f32[64,128]{1,0:T(8,128)S(1)}, f32[64,128]{1,0:T(8,128)S(1)}, u32[]{:S(2)}, u32[]{:S(2)}) collective-permute-start(f32[64,128]{1,0:T(8,128)S(1)} %get-tuple-element.59), channel_id=1, source_target_pairs={{0,16},{16,0},{32,48},{48,32},{64,80},{80,64},{96,112},{112,96},{1... | collective-permute-start | bytes 98312 | tf_op jit(solution)/shard_map/ppermute | solution.py:487
  76.5 1.0 %output.1 = (bf16[1024,128]{1,0:T(8,128)(2,1)}, bf16[1024,128]{1,0:T(8,128)(2,1)}, f32[8,128]{1,0:T(8,128)S(1)}) custom-call(f32[1280,128]{1,0:T(8,128)S(1)} %get-tuple-element.50.attn_ref, f32[256,128]{1,0:T(8,128)S(1)} %get-tuple-element.52.aux_ref, bf16[1024,128]{1,0:T(8,128)(2,1)S(1)} %copy-done.1, f32[1,128]{1,0:T(1,128)S(1)} %get-tuple-element.49.gain_ref, ...), custom_call_target="tpu_custom_call" | custom-call | flops 2000000 | bytes 2000000 | tf_op jit(solution)/shard_map/output/pallas_call | solution.py:413
  77.5 0.0 collective-permute-done.2.got_ref
  77.6 14.8 %all_to_all.23.got_ref = f32[8,64,128]{2,1,0:T(8,128)S(1)} all-to-all(f32[8,64,128]{2,1,0:T(8,128)S(1)} %get-tuple-element.61), channel_id=1, replica_groups={{0,32,64,96,128,160,192,224},{16,48,80,112,144,176,208,240},{1,33,65,97..., dimensions={0} | all-to-all | bytes 524288 | tf_op jit(solution)/shard_map/all_to_all | solution.py:426
  92.3 0.1 suffix.1
  92.4 2.4 %collective-permute-start.3 = (f32[64,128]{1,0:T(8,128)S(1)}, f32[64,128]{1,0:T(8,128)S(1)}, u32[]{:S(2)}, u32[]{:S(2)}) collective-permute-start(f32[64,128]{1,0:T(8,128)S(1)} %get-tuple-element.65), channel_id=1, source_target_pairs={{0,16},{16,0},{32,48},{48,32},{64,80},{80,64},{96,112},{112,96},{1... | collective-permute-start | bytes 98312 | tf_op jit(solution)/shard_map/ppermute | solution.py:508
  94.8 2.5 %backward.1 = (bf16[1024,128]{1,0:T(8,128)(2,1)}, f32[1024,128]{1,0:T(8,128)S(1)}, f32[1024,128]{1,0:T(8,128)S(1)}) custom-call(bf16[1024,128]{1,0:T(8,128)(2,1)S(1)} %copy-done, bf16[1024,128]{1,0:T(8,128)(2,1)S(1)} %get-tuple-element.37.k_ref, bf16[1024,128]{1,0:T(8,128)(2,1)S(1)} %get-tuple-element.38.v_ref, ...), custom_call_target="tpu_custom_call" | custom-call | flops 2000000 | bytes 2000000 | tf_op jit(solution)/shard_map/backward/pallas_call | solution.py:413
  97.2 0.0 collective-permute-done.3.got_ref
  97.2 1.2 %finish.1 = (bf16[1024,128]{1,0:T(8,128)(2,1)}, bf16[1024,128]{1,0:T(8,128)(2,1)}) custom-call(bf16[1024,128]{1,0:T(8,128)(2,1)S(1)} %get-tuple-element.37.k_ref, bf16[1024,128]{1,0:T(8,128)(2,1)S(1)} %get-tuple-element.38.v_ref, f32[1024,128]{1,0:T(8,128)S(1)} %get-tuple-element.56.gk_ref, f32[1024,128]{1,0:T(8,128)S(1)} %get-tuple-element.57.gv_ref, ...), custom_call_target="tpu_custom_call" | custom-call | flops 2000000 | bytes 2000000 | tf_op jit(solution)/shard_map/finish/pallas_call | solution.py:413
  (7 shorter events, 0.1 us)
Async XLA Ops:
  0.6 18.1 %copy-start = (bf16[1024,128]{1,0:T(8,128)(2,1)S(1)}, bf16[1024,128]{1,0:T(8,128)(2,1)}, u32[]{:S(2)}) copy-start(bf16[1024,128]{1,0:T(8,128)(2,1)} %q_ref.7) | copy-start | bytes 786436
  2.7 17.0 %collective-permute-start = (f32[72,128]{1,0:T(8,128)S(1)}, f32[72,128]{1,0:T(8,128)S(1)}, u32[]{:S(2)}, u32[]{:S(2)}) collective-permute-start(f32[72,128]{1,0:T(8,128)S(1)} %get-tuple-element.42), channel_id=1, source_target_pairs={{0,16},{16,0},{32,48},{48,32},{64,80},{80,64},{96,112},{112,96},{1... | collective-permute-start | bytes 110600 | tf_op jit(solution)/shard_map/ppermute | solution.py:457
  19.7 18.2 %copy-start.2 = (bf16[1024,128]{1,0:T(8,128)(2,1)S(1)}, bf16[1024,128]{1,0:T(8,128)(2,1)}, u32[]{:S(2)}) copy-start(bf16[1024,128]{1,0:T(8,128)(2,1)} %gout_ref.1) | copy-start | bytes 786436
  34.9 3.0 %copy-start.1 = (bf16[1024,128]{1,0:T(8,128)(2,1)S(1)}, bf16[1024,128]{1,0:T(8,128)(2,1)}, u32[]{:S(2)}) copy-start(bf16[1024,128]{1,0:T(8,128)(2,1)} %gin_ref.1) | copy-start | bytes 786436
  35.0 3.7 %collective-permute-start.1 = (f32[64,128]{1,0:T(8,128)S(1)}, f32[64,128]{1,0:T(8,128)S(1)}, u32[]{:S(2)}, u32[]{:S(2)}) collective-permute-start(f32[64,128]{1,0:T(8,128)S(1)} %get-tuple-element.47), channel_id=1, source_target_pairs={{0,16},{16,0},{32,48},{48,32},{64,80},{80,64},{96,112},{112,96},{1... | collective-permute-start | bytes 98312 | tf_op jit(solution)/shard_map/ppermute | solution.py:470
  70.5 7.0 %collective-permute-start.2 = (f32[64,128]{1,0:T(8,128)S(1)}, f32[64,128]{1,0:T(8,128)S(1)}, u32[]{:S(2)}, u32[]{:S(2)}) collective-permute-start(f32[64,128]{1,0:T(8,128)S(1)} %get-tuple-element.59), channel_id=1, source_target_pairs={{0,16},{16,0},{32,48},{48,32},{64,80},{80,64},{96,112},{112,96},{1... | collective-permute-start | bytes 98312 | tf_op jit(solution)/shard_map/ppermute | solution.py:487
  92.4 4.8 %collective-permute-start.3 = (f32[64,128]{1,0:T(8,128)S(1)}, f32[64,128]{1,0:T(8,128)S(1)}, u32[]{:S(2)}, u32[]{:S(2)}) collective-permute-start(f32[64,128]{1,0:T(8,128)S(1)} %get-tuple-element.65), channel_id=1, source_target_pairs={{0,16},{16,0},{32,48},{48,32},{64,80},{80,64},{96,112},{112,96},{1... | collective-permute-start | bytes 98312 | tf_op jit(solution)/shard_map/ppermute | solution.py:508

commit v4 on v3

--- a/solution.py
+++ b/solution.py
@@ -101,7 +101,7 @@
 
 
 def states_kernel(
-    k_hbm, v_hbm, rates_hbm, gain_hbm, send_ref, keep_ref, entry_ref, sums_ref, turned_ref, gain_ref, k_ref, v_ref,
+    k_hbm, v_hbm, q_hbm, rates_hbm, gain_hbm, send_ref, keep_ref, entry_ref, sums_ref, turned_ref, gain_ref, k_ref, v_ref, q_ref,
     rates_ref, state_ref, sems,
 ):
     length = k_ref.shape[0]
@@ -113,6 +113,7 @@
         copies.append(pltpu.make_async_copy(v_hbm.at[rows], v_ref.at[rows], sems.at[2 * b + 1]))
         copies.append(pltpu.make_async_copy(k_hbm.at[rows], k_ref.at[rows], sems.at[2 * b + 2]))
     copies.append(pltpu.make_async_copy(gain_hbm, gain_ref, sems.at[2 * blocks + 1]))
+    copies.append(pltpu.make_async_copy(q_hbm, q_ref, sems.at[2 * blocks + 2]))
     for copy in copies:
         copy.start()
     copies[0].wait()
@@ -147,6 +148,7 @@
     keep_ref[half:, :] = spread
     send_ref[:half, :] = state_ref[pl.ds(pl.multiple_of((1 - core) * half, half), half), :]
     send_ref[half:, :] = spread
+    copies[-2].wait()
     copies[-1].wait()
 
 
@@ -215,7 +217,7 @@
     )
 
 
-def local_kernel(q_ref, k_ref, v_ref, sums_ref, turned_ref, out_ref):
+def local_kernel(q_ref, k_ref, v_ref, sums_ref, turned_ref, out_ref, table_ref, weights_ref):
     length = q_ref.shape[0]
     sums, turned = sums_ref[...], turned_ref[...]
     for b in range(length // BLOCK):
@@ -224,11 +226,20 @@
             rows = slice(at + i * TILE, at + (i + 1) * TILE)
             cols = slice(at, at + (i + 1) * TILE)
             scores = dot(q_ref[rows, :], k_ref[cols, :], 1, 1)
-            weights = (scores * weights_tile(sums, turned, at, i)).astype(bf16)
+            table = weights_tile(sums, turned, at, i)
+            weights = (scores * table).astype(bf16)
+            table_ref[rows, : (i + 1) * TILE] = table
+            weights_ref[rows, : (i + 1) * TILE] = weights
             out_ref[rows, :] = dot(weights, v_ref[cols, :])
 
 
-def gate_kernel(gate_ref, grad_ref, gain_ref, signal_ref):
+def gate_kernel(gate_ref, grad_ref, gain_ref, q_ref, sums_ref, signal_ref, fronted_ref):
+    front = jnp.exp(sums_ref[...])
+    for r in range(q_ref.shape[0] // CHUNK):
+        at = slice(r * CHUNK, (r + 1) * CHUNK)
+        parts = split3(q_ref[at, :].astype(f32).T * front[r : r + 1, :])
+        for n, piece in enumerate(parts):
+            fronted_ref[n * HEAD_DIM : (n + 1) * HEAD_DIM, at] = piece
     prob = jax.nn.sigmoid(gate_ref[...].astype(f32))
     signal_ref[...] = grad_ref[...].astype(f32) * prob * gain_ref[...]
 
@@ -277,13 +288,13 @@
 
 
 def grad_kernel(
-    n_exp, width, got_ref, attn_ref, signal_ref, q_ref, sums_ref, turned_ref,
+    n_exp, width, got_ref, attn_ref, signal_ref, fronted_ref, sums_ref,
     grad_ref, keep_ref, send_ref, aux_ref, state_ref,
 ):
-    length = q_ref.shape[0]
+    length = signal_ref.shape[0]
     half = HEAD_DIM // 2
     blocks = length // BLOCK
-    sums, turned = sums_ref[...], turned_ref[...]
+    sums = sums_ref[...]
     total = got_ref[0]
     for j in range(1, n_exp):
         total = total + got_ref[j]
@@ -299,8 +310,8 @@
         alo = column(both[:, 8:], at, BLOCK)
         grad = (inv * signal_ref[rows, :] - alo * attn_ref[rows, :]).astype(bf16)
         grad_ref[rows, :] = grad
-        front = column(turned, at, BLOCK, 1)
-        update = exact_outer(q_ref[rows, :], grad.astype(f32) * front)
+        parts = dot(fronted_ref[:, rows], grad)
+        update = parts[:HEAD_DIM] + (parts[HEAD_DIM : 2 * HEAD_DIM] + parts[2 * HEAD_DIM :])
         state = update if state is None else jnp.exp(last_of(sums, b)) * state + update
         if b:
             aux_ref[(b - 1) * HEAD_DIM : b * HEAD_DIM, :] = state
@@ -311,10 +322,10 @@
 
 
 def output_kernel(
-    attn_ref, aux_ref, gin_ref, gain_ref, gout_ref, layer_hbm, gate_hbm, done_ref, layer_ref, gate_ref, sems,
+    attn_ref, aux_ref, gin_ref, gain_ref, gout_ref, k_ref, v_ref, turned_ref,
+    layer_hbm, gate_hbm, base_k_ref, base_v_ref, layer_ref, gate_ref, sems,
 ):
     length = gout_ref.shape[0]
-    done_ref[...] = jnp.zeros_like(done_ref)
     both = aux_ref[aux_ref.shape[0] - HEAD_DIM :, :16]
     copies = []
     for b in range(length // BLOCK):
@@ -328,42 +339,41 @@
         gate_ref[rows, :] = (gout_ref[rows, :].astype(f32) * layer * (1.0 - prob)).astype(bf16)
         copies.append(pltpu.make_async_copy(gate_ref.at[part], gate_hbm.at[part], sems.at[2 * b + 1]))
         copies[-1].start()
+    turned = turned_ref[...]
+    for b in range(length // BLOCK - 1):
+        rows = slice(b * BLOCK, (b + 1) * BLOCK)
+        tail = column(turned, b * BLOCK, BLOCK, 2)
+        later = aux_ref[b * HEAD_DIM : (b + 1) * HEAD_DIM, :]
+        base_k_ref[rows, :] = tail * exact_dot(v_ref[rows, :], later, True)
+        base_v_ref[rows, :] = tail * exact_dot(k_ref[rows, :], later)
     for copy in copies:
         copy.wait()
 
 
 def backward_kernel(
-    q_ref, k_ref, v_ref, grad_ref, attn_ref, aux_ref, sums_ref, turned_ref,
+    q_ref, k_ref, v_ref, grad_ref, attn_ref, base_k_ref, base_v_ref, table_ref, weights_ref, turned_ref,
     gq_hbm, gk_ref, gv_ref, gq_ref, sems,
 ):
     length = q_ref.shape[0]
     blocks = length // BLOCK
-    sums, turned = sums_ref[...], turned_ref[...]
+    turned = turned_ref[...]
     copies = []
     for b in range(blocks):
         at = b * BLOCK
-        whole = slice(at, at + BLOCK)
-        later = None
-        if b < blocks - 1:
-            later = aux_ref[b * HEAD_DIM : (b + 1) * HEAD_DIM, :]
         entering = attn_ref[length + b * HEAD_DIM : length + (b + 1) * HEAD_DIM, :]
         for i in range(BLOCK // TILE):
             rows = slice(at + i * TILE, at + (i + 1) * TILE)
             cols = slice(at, at + (i + 1) * TILE)
-            table = weights_tile(sums, turned, at, i)
             q, g = q_ref[rows, :], grad_ref[rows, :]
-            wq = (dot(q, k_ref[cols, :], 1, 1) * table).astype(bf16)
+            wq = weights_ref[rows, : (i + 1) * TILE]
+            table = table_ref[rows, : (i + 1) * TILE]
             gw = (dot(g, v_ref[cols, :], 1, 1) * table).astype(bf16)
             front = column(turned, at + i * TILE, TILE, 1)
             grad_q = dot(gw, k_ref[cols, :]) + front * exact_dot(g, entering, True)
             gq_ref[rows, :] = grad_q.astype(bf16)
             add_k, add_v = dot(gw, q, 0, 0), dot(wq, g, 0, 0)
-            if later is not None:
-                tail = column(turned, at + i * TILE, TILE, 2)
-                more_k = tail * exact_dot(v_ref[rows, :], later, True)
-                more_v = tail * exact_dot(k_ref[rows, :], later)
-            else:
-                more_k = more_v = 0.0
+            more_k = base_k_ref[rows, :] if b < blocks - 1 else 0.0
+            more_v = base_v_ref[rows, :] if b < blocks - 1 else 0.0
             if i:
                 old = slice(at, at + i * TILE)
                 gk_ref[old, :] += add_k[: i * TILE, :]
@@ -440,29 +450,35 @@
     full, half = ((length, HEAD_DIM), f32), ((length, HEAD_DIM), bf16)
     piece, marked = ((part, HEAD_DIM), f32), ((part + 8, HEAD_DIM), f32)
 
-    sent, keep, entry, sums, turned, gain, held_k, held_v = call(
+    sent, keep, entry, sums, turned, gain, held_k, held_v, held_q = call(
         states_kernel, "states",
         [marked, marked, ((blocks - 1, HEAD_DIM, HEAD_DIM), f32), ((chunks, CHUNK), f32),
-         ((CHUNK, 4 * chunks), f32), ((1, HEAD_DIM), f32), half, half],
+         ((CHUNK, 4 * chunks), f32), ((1, HEAD_DIM), f32), half, half, half],
         *(
             pltpu.with_memory_space_constraint(a, pltpu.HBM)
-            for a in (key_rows, value_rows, rates, norm_gain.reshape(1, HEAD_DIM))
+            for a in (key_rows, value_rows, queries, rates, norm_gain.reshape(1, HEAD_DIM))
         ),
         hbm_in=True, cost=1e7,
         scratch=[
             pltpu.VMEM((chunks, CHUNK), f32), pltpu.VMEM((HEAD_DIM, HEAD_DIM), f32),
-            pltpu.SemaphoreType.DMA((2 * blocks + 2,)),
+            pltpu.SemaphoreType.DMA((2 * blocks + 3,)),
         ],
     )
     got = lax.ppermute(sent, "ctx", pairs)
-    (local,) = call(local_kernel, "local", [full], queries, held_k, held_v, sums, turned)
+    local, table, weights = call(
+        local_kernel, "local", [full, ((length, BLOCK), f32), ((length, BLOCK), bf16)],
+        held_q, held_k, held_v, sums, turned,
+    )
     sent, first, totals = call(
         partial(pair_kernel, n_chip), "pair",
         [((n_chip, part + 8, HEAD_DIM), f32), piece, ((16, HEAD_DIM), f32)],
         keep, got, local, hbm_last=True,
     )
     got = exchange(sent, "ctx", lines)
-    (signal,) = call(gate_kernel, "gate", [full], gate_input, grad_output, gain)
+    signal, fronted = call(
+        gate_kernel, "gate", [full, ((3 * HEAD_DIM, length), bf16)],
+        gate_input, grad_output, gain, held_q, sums,
+    )
     keep, sent, chips = call(
         partial(prefix_kernel, n_chip), "prefix", [piece, piece, ((n_chip, HEAD_DIM), f32)],
         got, first, totals,
@@ -471,7 +487,7 @@
     attn, sent = call(
         partial(attn_kernel, n_section), "attn",
         [((length + blocks * HEAD_DIM, HEAD_DIM), f32), ((n_section, 16, CHUNK), f32)],
-        queries, local, keep, got, entry, sums, turned, signal,
+        held_q, local, keep, got, entry, sums, turned, signal,
     )
     got = exchange(sent, "section")
     (sent,) = call(
@@ -481,12 +497,14 @@
     grad, keep, sent, aux = call(
         partial(grad_kernel, n_exp, width), "grad",
         [half, piece, piece, ((blocks * HEAD_DIM, HEAD_DIM), f32)],
-        got, attn, signal, queries, sums, turned,
+        got, attn, signal, fronted, sums,
         scratch=[pltpu.VMEM((HEAD_DIM, HEAD_DIM), f32)],
     )
     got = lax.ppermute(sent, "ctx", pairs)
-    layer_out, grad_gate, done = call(
-        output_kernel, "output", [half, half, ((8, HEAD_DIM), f32)], attn, aux, gate_input, gain, grad_output, hbm_out=2,
+    early = ((length - BLOCK, HEAD_DIM), f32)
+    layer_out, grad_gate, base_k, base_v = call(
+        output_kernel, "output", [half, half, early, early],
+        attn, aux, gate_input, gain, grad_output, held_k, held_v, turned, hbm_out=2,
         scratch=[
             pltpu.VMEM((length, HEAD_DIM), bf16), pltpu.VMEM((length, HEAD_DIM), bf16),
             pltpu.SemaphoreType.DMA((2 * blocks,)),
@@ -494,12 +512,12 @@
     )
     sent, second = call(
         partial(back_pair_kernel, n_chip), "back_pair",
-        [((n_chip, part, HEAD_DIM), f32), piece], keep, got, totals, done,
+        [((n_chip, part, HEAD_DIM), f32), piece], keep, got, totals, base_v, hbm_last=True,
     )
     got = exchange(sent, "ctx", lines)
     grad_q, local_k, local_v = call(
         backward_kernel, "backward", [half, full, full],
-        queries, held_k, held_v, grad, attn, aux, sums, turned, hbm_out=1,
+        held_q, held_k, held_v, grad, attn, base_k, base_v, table, weights, turned, hbm_out=1,
         scratch=[pltpu.VMEM((length, HEAD_DIM), bf16), pltpu.SemaphoreType.DMA((blocks,))],
     )
     keep, sent = call(

time: 98.8 us -> 98.4 us (level)
  no operation moved by 1% of the time
where the time goes in v4:
time: 98.4 us; the launch traced here: 98 us
  blocking collectives  60 us (61%)
  starting transfers between devices  27 us (27%)
  Pallas kernels  9.77 us (10%)
    all_to_all x4, blocking collectives, exchange(): return lax.all_to_all(x, axis, 0, 0, axis_index_groups=groups)  60 us
    ppermute x4, starting transfers between devices, on_device(): got = lax.ppermute(sent, 'ctx', pairs)  27 us
    pallas_call x13, Pallas kernels, call(): pl.pallas_call(kernel, out_shape=shapes, in_specs=[pl.BlockSpec(memory_sp...  9.77 us
  transfers between devices with their start and end apart: 4, of which 1 were waited for; matrix products, arithmetic and copies ran while one was open for 0% of the time, Pallas kernels for 5%

profile of v4, /device:TPU:1, one launch (start us, length us, event | category | flops | bytes accessed | tf_op | source)
XLA Modules:
  0.0 98.0 jit_solution(11023873254913132763)
XLA Ops:
  0.6 0.0 copy-start
  0.6 0.0 copy-start.1
  0.7 2.1 %states.1 = (f32[72,128]{1,0:T(8,128)S(1)}, f32[72,128]{1,0:T(8,128)S(1)}, f32[1,128,128]{2,1,0:T(8,128)S(1)}, f32[8,128]{1,0:T(8,128)S(1)}, f32[128,32]{1,0:T(8...) custom-call(bf16[1024,128]{1,0:T(8,128)(2,1)} %k_hbm.1, ...), custom_call_target="tpu_custom_call" | custom-call | flops 10000000 | bytes 10000000 | tf_op jit(solution)/shard_map/states/pallas_call | solution.py:423
  2.7 16.0 %collective-permute-start = (f32[72,128]{1,0:T(8,128)S(1)}, f32[72,128]{1,0:T(8,128)S(1)}, u32[]{:S(2)}, u32[]{:S(2)}) collective-permute-start(f32[72,128]{1,0:T(8,128)S(1)} %get-tuple-element.51), channel_id=1, source_target_pairs={{0,16},{16,0},{32,48},{48,32},{64,80},{80,64},{96,112},{112,96},{1... | collective-permute-start | bytes 110600 | tf_op jit(solution)/shard_map/ppermute | solution.py:467
  18.7 1.0 local.1
  19.7 0.0 collective-permute-done.got_ref
  19.8 15.1 %all_to_all.20.got_ref = f32[8,72,128]{2,1,0:T(8,128)S(1)} all-to-all(f32[8,72,128]{2,1,0:T(8,128)S(1)} %get-tuple-element.52), channel_id=1, replica_groups={{0,32,64,96,128,160,192,224},{16,48,80,112,144,176,208,240},{1,33,65,97..., dimensions={0} | all-to-all | bytes 589824 | tf_op jit(solution)/shard_map/all_to_all | solution.py:436
  34.9 0.1 prefix.1
  34.9 2.7 %collective-permute-start.1 = (f32[64,128]{1,0:T(8,128)S(1)}, f32[64,128]{1,0:T(8,128)S(1)}, u32[]{:S(2)}, u32[]{:S(2)}) collective-permute-start(f32[64,128]{1,0:T(8,128)S(1)} %get-tuple-element.56), channel_id=1, source_target_pairs={{0,16},{16,0},{32,48},{48,32},{64,80},{80,64},{96,112},{112,96},{1... | collective-permute-start | bytes 98312 | tf_op jit(solution)/shard_map/ppermute | solution.py:486
  37.7 0.4 gate.1
  38.1 0.4 collective-permute-done.1.got_ref
  38.5 0.7 attn.1
  39.2 6.7 %all_to_all.21.got_ref = f32[4,16,128]{2,1,0:T(8,128)S(1)} all-to-all(f32[4,16,128]{2,1,0:T(8,128)S(1)} %get-tuple-element.61), channel_id=1, replica_groups=mesh['section'=4,'ctx'=16,'exp'=16] {'section'}, dimensions={0} | all-to-all | bytes 65536 | tf_op jit(solution)/shard_map/all_to_all | solution.py:436
  45.9 23.4 %all_to_all.22.got_ref = f32[16,16,128]{2,1,0:T(8,128)S(1)} all-to-all(f32[16,16,128]{2,1,0:T(8,128)S(1)} %relay.1), channel_id=1, replica_groups=mesh['section'=4,'ctx'=16,'exp'=16] {'exp'}, dimensions={0} | all-to-all | bytes 262144 | tf_op jit(solution)/shard_map/all_to_all | solution.py:436
  69.3 0.9 grad.1
  70.2 5.9 %collective-permute-start.2 = (f32[64,128]{1,0:T(8,128)S(1)}, f32[64,128]{1,0:T(8,128)S(1)}, u32[]{:S(2)}, u32[]{:S(2)}) collective-permute-start(f32[64,128]{1,0:T(8,128)S(1)} %get-tuple-element.74), channel_id=1, source_target_pairs={{0,16},{16,0},{32,48},{48,32},{64,80},{80,64},{96,112},{112,96},{1... | collective-permute-start | bytes 98312 | tf_op jit(solution)/shard_map/ppermute | solution.py:503
  76.2 1.1 %output.1 = (bf16[1024,128]{1,0:T(8,128)(2,1)}, bf16[1024,128]{1,0:T(8,128)(2,1)}, f32[512,128]{1,0:T(8,128)S(1)}, f32[512,128]{1,0:T(8,128)S(1)}) custom-call(f32[1280,128]{1,0:T(8,128)S(1)} %get-tuple-element.60.attn_ref, f32[256,128]{1,0:T(8,128)S(1)} %get-tuple-element.63.aux_ref, bf16[1024,128]{1,0:T(8,128)(2,1)S(1)} %copy-done, ...), custom_call_target="tpu_custom_call" | custom-call | flops 2000000 | bytes 2000000 | tf_op jit(solution)/shard_map/output/pallas_call | solution.py:423
  77.2 0.0 collective-permute-done.2.got_ref
  77.3 14.8 %all_to_all.23.got_ref = f32[8,64,128]{2,1,0:T(8,128)S(1)} all-to-all(f32[8,64,128]{2,1,0:T(8,128)S(1)} %get-tuple-element.75), channel_id=1, replica_groups={{0,32,64,96,128,160,192,224},{16,48,80,112,144,176,208,240},{1,33,65,97..., dimensions={0} | all-to-all | bytes 524288 | tf_op jit(solution)/shard_map/all_to_all | solution.py:436
  92.1 0.1 suffix.1
  92.1 2.4 %collective-permute-start.3 = (f32[64,128]{1,0:T(8,128)S(1)}, f32[64,128]{1,0:T(8,128)S(1)}, u32[]{:S(2)}, u32[]{:S(2)}) collective-permute-start(f32[64,128]{1,0:T(8,128)S(1)} %get-tuple-element.79), channel_id=1, source_target_pairs={{0,16},{16,0},{32,48},{48,32},{64,80},{80,64},{96,112},{112,96},{1... | collective-permute-start | bytes 98312 | tf_op jit(solution)/shard_map/ppermute | solution.py:526
  94.5 2.3 %backward.1 = (bf16[1024,128]{1,0:T(8,128)(2,1)}, f32[1024,128]{1,0:T(8,128)S(1)}, f32[1024,128]{1,0:T(8,128)S(1)}) custom-call(bf16[1024,128]{1,0:T(8,128)(2,1)S(1)} %get-tuple-element.44.q_ref, bf16[1024,128]{1,0:T(8,128)(2,1)S(1)} %get-tuple-element.45.k_ref, bf16[1024,128]{1,0:T(8,128)(2,1)S(1)} %get-tuple-element.46.v_ref, ...), custom_call_target="tpu_custom_call" | custom-call | flops 2000000 | bytes 2000000 | tf_op jit(solution)/shard_map/backward/pallas_call | solution.py:423
  96.8 0.0 collective-permute-done.3.got_ref
  96.8 1.2 %finish.1 = (bf16[1024,128]{1,0:T(8,128)(2,1)}, bf16[1024,128]{1,0:T(8,128)(2,1)}) custom-call(bf16[1024,128]{1,0:T(8,128)(2,1)S(1)} %get-tuple-element.45.k_ref, bf16[1024,128]{1,0:T(8,128)(2,1)S(1)} %get-tuple-element.46.v_ref, f32[1024,128]{1,0:T(8,128)S(1)} %get-tuple-element.71.gk_ref, f32[1024,128]{1,0:T(8,128)S(1)} %get-tuple-element.72.gv_ref, ...), custom_call_target="tpu_custom_call" | custom-call | flops 2000000 | bytes 2000000 | tf_op jit(solution)/shard_map/finish/pallas_call | solution.py:423
  (5 shorter events, 0.1 us)
Async XLA Ops:
  0.6 37.0 %copy-start = (bf16[1024,128]{1,0:T(8,128)(2,1)S(1)}, bf16[1024,128]{1,0:T(8,128)(2,1)}, u32[]{:S(2)}) copy-start(bf16[1024,128]{1,0:T(8,128)(2,1)} %gin_ref.1) | copy-start | bytes 786436
  0.6 37.0 %copy-start.1 = (bf16[1024,128]{1,0:T(8,128)(2,1)S(1)}, bf16[1024,128]{1,0:T(8,128)(2,1)}, u32[]{:S(2)}) copy-start(bf16[1024,128]{1,0:T(8,128)(2,1)} %gout_ref.1) | copy-start | bytes 786436
  2.7 17.0 %collective-permute-start = (f32[72,128]{1,0:T(8,128)S(1)}, f32[72,128]{1,0:T(8,128)S(1)}, u32[]{:S(2)}, u32[]{:S(2)}) collective-permute-start(f32[72,128]{1,0:T(8,128)S(1)} %get-tuple-element.51), channel_id=1, source_target_pairs={{0,16},{16,0},{32,48},{48,32},{64,80},{80,64},{96,112},{112,96},{1... | collective-permute-start | bytes 110600 | tf_op jit(solution)/shard_map/ppermute | solution.py:467
  34.9 3.6 %collective-permute-start.1 = (f32[64,128]{1,0:T(8,128)S(1)}, f32[64,128]{1,0:T(8,128)S(1)}, u32[]{:S(2)}, u32[]{:S(2)}) collective-permute-start(f32[64,128]{1,0:T(8,128)S(1)} %get-tuple-element.56), channel_id=1, source_target_pairs={{0,16},{16,0},{32,48},{48,32},{64,80},{80,64},{96,112},{112,96},{1... | collective-permute-start | bytes 98312 | tf_op jit(solution)/shard_map/ppermute | solution.py:486
  70.2 7.0 %collective-permute-start.2 = (f32[64,128]{1,0:T(8,128)S(1)}, f32[64,128]{1,0:T(8,128)S(1)}, u32[]{:S(2)}, u32[]{:S(2)}) collective-permute-start(f32[64,128]{1,0:T(8,128)S(1)} %get-tuple-element.74), channel_id=1, source_target_pairs={{0,16},{16,0},{32,48},{48,32},{64,80},{80,64},{96,112},{112,96},{1... | collective-permute-start | bytes 98312 | tf_op jit(solution)/shard_map/ppermute | solution.py:503
  92.1 4.7 %collective-permute-start.3 = (f32[64,128]{1,0:T(8,128)S(1)}, f32[64,128]{1,0:T(8,128)S(1)}, u32[]{:S(2)}, u32[]{:S(2)}) collective-permute-start(f32[64,128]{1,0:T(8,128)S(1)} %get-tuple-element.79), channel_id=1, source_target_pairs={{0,16},{16,0},{32,48},{48,32},{64,80},{80,64},{96,112},{112,96},{1... | collective-permute-start | bytes 98312 | tf_op jit(solution)/shard_map/ppermute | solution.py:526

commit v5 on v4

--- a/solution.py
+++ b/solution.py
@@ -233,10 +233,13 @@
             out_ref[rows, :] = dot(weights, v_ref[cols, :])
 
 
-def gate_kernel(gate_ref, grad_ref, gain_ref, q_ref, sums_ref, signal_ref, fronted_ref):
+def gate_kernel(
+    gate_ref, grad_ref, gain_ref, q_ref, sums_ref, turned_ref, signal_ref, fronted_ref, front_ref,
+):
     front = jnp.exp(sums_ref[...])
     for r in range(q_ref.shape[0] // CHUNK):
         at = slice(r * CHUNK, (r + 1) * CHUNK)
+        front_ref[at, :] = jnp.broadcast_to(column(turned_ref[...], r * CHUNK, CHUNK, 1), (CHUNK, CHUNK))
         parts = split3(q_ref[at, :].astype(f32).T * front[r : r + 1, :])
         for n, piece in enumerate(parts):
             fronted_ref[n * HEAD_DIM : (n + 1) * HEAD_DIM, at] = piece
@@ -245,21 +248,21 @@
 
 
 def row_sums(x):
-    down = lax.broadcasted_iota(jnp.int32, (CHUNK, CHUNK), 0)
-    across = lax.broadcasted_iota(jnp.int32, (CHUNK, CHUNK), 1)
-    pieces = []
-    for r in range(x.shape[0] // CHUNK):
-        sums = jnp.sum(x[r * CHUNK : (r + 1) * CHUNK, :], axis=1, keepdims=True)
-        pieces.append(jnp.sum(jnp.where(down == across, sums, 0.0), axis=0, keepdims=True))
-    return jnp.concatenate(pieces, axis=0)
+    return jnp.concatenate(
+        [
+            jnp.sum(x[r * CHUNK : (r + 1) * CHUNK, :].T, axis=0, keepdims=True)
+            for r in range(x.shape[0] // CHUNK)
+        ],
+        axis=0,
+    )
 
 
 def attn_kernel(
-    n_section, q_ref, local_ref, keep_ref, got_ref, entry_ref, sums_ref, turned_ref, signal_ref,
+    n_section, q_ref, local_ref, keep_ref, got_ref, entry_ref, sums_ref, front_ref, signal_ref,
     attn_ref, send_ref,
 ):
     length = q_ref.shape[0]
-    sums, turned = sums_ref[...], turned_ref[...]
+    sums = sums_ref[...]
     start = whole_state(keep_ref, got_ref)
     state, gone = start, jnp.zeros((1, 1), f32)
     for b in range(length // BLOCK):
@@ -268,8 +271,7 @@
         if b:
             state = entry_ref[b - 1] + jnp.exp(gone) * start
         attn_ref[length + b * HEAD_DIM : length + (b + 1) * HEAD_DIM, :] = state
-        front = column(turned, at, BLOCK, 1)
-        attn_ref[rows, :] = local_ref[rows, :] + front * exact_dot(q_ref[rows, :], state)
+        attn_ref[rows, :] = local_ref[rows, :] + front_ref[rows, :] * exact_dot(q_ref[rows, :], state)
         gone = gone + last_of(sums, b)
     attn = attn_ref[:length, :]
     squares = row_sums(attn * attn)
@@ -323,22 +325,17 @@
 
 def output_kernel(
     attn_ref, aux_ref, gin_ref, gain_ref, gout_ref, k_ref, v_ref, turned_ref,
-    layer_hbm, gate_hbm, base_k_ref, base_v_ref, layer_ref, gate_ref, sems,
+    layer_ref, gate_ref, base_k_ref, base_v_ref,
 ):
     length = gout_ref.shape[0]
     both = aux_ref[aux_ref.shape[0] - HEAD_DIM :, :16]
-    copies = []
     for b in range(length // BLOCK):
-        rows, part = slice(b * BLOCK, (b + 1) * BLOCK), pl.ds(b * BLOCK, BLOCK)
+        rows = slice(b * BLOCK, (b + 1) * BLOCK)
         scaled = attn_ref[rows, :] * column(both, b * BLOCK, BLOCK) * gain_ref[...]
         prob = jax.nn.sigmoid(gin_ref[rows, :].astype(f32))
         layer = scaled * prob
         layer_ref[rows, :] = layer.astype(bf16)
-        copies.append(pltpu.make_async_copy(layer_ref.at[part], layer_hbm.at[part], sems.at[2 * b]))
-        copies[-1].start()
         gate_ref[rows, :] = (gout_ref[rows, :].astype(f32) * layer * (1.0 - prob)).astype(bf16)
-        copies.append(pltpu.make_async_copy(gate_ref.at[part], gate_hbm.at[part], sems.at[2 * b + 1]))
-        copies[-1].start()
     turned = turned_ref[...]
     for b in range(length // BLOCK - 1):
         rows = slice(b * BLOCK, (b + 1) * BLOCK)
@@ -346,18 +343,20 @@
         later = aux_ref[b * HEAD_DIM : (b + 1) * HEAD_DIM, :]
         base_k_ref[rows, :] = tail * exact_dot(v_ref[rows, :], later, True)
         base_v_ref[rows, :] = tail * exact_dot(k_ref[rows, :], later)
-    for copy in copies:
-        copy.wait()
 
 
 def backward_kernel(
-    q_ref, k_ref, v_ref, grad_ref, attn_ref, base_k_ref, base_v_ref, table_ref, weights_ref, turned_ref,
-    gq_hbm, gk_ref, gv_ref, gq_ref, sems,
+    q_ref, k_ref, v_ref, grad_ref, attn_ref, base_k_ref, base_v_ref, table_ref, weights_ref, front_ref,
+    layer_ref, gate_ref, layer_hbm, gate_hbm, gq_ref, gk_ref, gv_ref, sems,
 ):
     length = q_ref.shape[0]
     blocks = length // BLOCK
-    turned = turned_ref[...]
-    copies = []
+    copies = [
+        pltpu.make_async_copy(layer_ref, layer_hbm, sems.at[0]),
+        pltpu.make_async_copy(gate_ref, gate_hbm, sems.at[1]),
+    ]
+    for copy in copies:
+        copy.start()
     for b in range(blocks):
         at = b * BLOCK
         entering = attn_ref[length + b * HEAD_DIM : length + (b + 1) * HEAD_DIM, :]
@@ -368,8 +367,7 @@
             wq = weights_ref[rows, : (i + 1) * TILE]
             table = table_ref[rows, : (i + 1) * TILE]
             gw = (dot(g, v_ref[cols, :], 1, 1) * table).astype(bf16)
-            front = column(turned, at + i * TILE, TILE, 1)
-            grad_q = dot(gw, k_ref[cols, :]) + front * exact_dot(g, entering, True)
+            grad_q = dot(gw, k_ref[cols, :]) + front_ref[rows, :] * exact_dot(g, entering, True)
             gq_ref[rows, :] = grad_q.astype(bf16)
             add_k, add_v = dot(gw, q, 0, 0), dot(wq, g, 0, 0)
             more_k = base_k_ref[rows, :] if b < blocks - 1 else 0.0
@@ -380,23 +378,21 @@
                 gv_ref[old, :] += add_v[: i * TILE, :]
             gk_ref[rows, :] = add_k[i * TILE :, :] + more_k
             gv_ref[rows, :] = add_v[i * TILE :, :] + more_v
-        part = pl.ds(at, BLOCK)
-        copies.append(pltpu.make_async_copy(gq_ref.at[part], gq_hbm.at[part], sems.at[b]))
-        copies[-1].start()
     for copy in copies:
         copy.wait()
 
 
 def finish_kernel(
-    k_ref, v_ref, gk_ref, gv_ref, keep_ref, got_ref, sums_ref, turned_ref, ok_hbm, ov_hbm,
-    ok_ref, ov_ref, sems,
+    k_ref, v_ref, gk_ref, gv_ref, keep_ref, got_ref, sums_ref, turned_ref, gq_ref,
+    ok_hbm, ov_hbm, oq_hbm, ok_ref, ov_ref, sems,
 ):
     length = k_ref.shape[0]
     blocks = length // BLOCK
     sums, turned = sums_ref[...], turned_ref[...]
     start = whole_state(keep_ref, got_ref)
     after = jnp.zeros((1, 1), f32)
-    copies = []
+    copies = [pltpu.make_async_copy(gq_ref, oq_hbm, sems.at[2 * blocks])]
+    copies[0].start()
     for b in reversed(range(blocks)):
         at = b * BLOCK
         rows = slice(at, at + BLOCK)
@@ -475,9 +471,9 @@
         keep, got, local, hbm_last=True,
     )
     got = exchange(sent, "ctx", lines)
-    signal, fronted = call(
-        gate_kernel, "gate", [full, ((3 * HEAD_DIM, length), bf16)],
-        gate_input, grad_output, gain, held_q, sums,
+    signal, fronted, front = call(
+        gate_kernel, "gate", [full, ((3 * HEAD_DIM, length), bf16), full],
+        gate_input, grad_output, gain, held_q, sums, turned,
     )
     keep, sent, chips = call(
         partial(prefix_kernel, n_chip), "prefix", [piece, piece, ((n_chip, HEAD_DIM), f32)],
@@ -487,7 +483,7 @@
     attn, sent = call(
         partial(attn_kernel, n_section), "attn",
         [((length + blocks * HEAD_DIM, HEAD_DIM), f32), ((n_section, 16, CHUNK), f32)],
-        held_q, local, keep, got, entry, sums, turned, signal,
+        held_q, local, keep, got, entry, sums, front, signal,
     )
     got = exchange(sent, "section")
     (sent,) = call(
@@ -504,32 +500,28 @@
     early = ((length - BLOCK, HEAD_DIM), f32)
     layer_out, grad_gate, base_k, base_v = call(
         output_kernel, "output", [half, half, early, early],
-        attn, aux, gate_input, gain, grad_output, held_k, held_v, turned, hbm_out=2,
-        scratch=[
-            pltpu.VMEM((length, HEAD_DIM), bf16), pltpu.VMEM((length, HEAD_DIM), bf16),
-            pltpu.SemaphoreType.DMA((2 * blocks,)),
-        ],
+        attn, aux, gate_input, gain, grad_output, held_k, held_v, turned,
     )
     sent, second = call(
         partial(back_pair_kernel, n_chip), "back_pair",
         [((n_chip, part, HEAD_DIM), f32), piece], keep, got, totals, base_v, hbm_last=True,
     )
     got = exchange(sent, "ctx", lines)
-    grad_q, local_k, local_v = call(
-        backward_kernel, "backward", [half, full, full],
-        held_q, held_k, held_v, grad, attn, base_k, base_v, table, weights, turned, hbm_out=1,
-        scratch=[pltpu.VMEM((length, HEAD_DIM), bf16), pltpu.SemaphoreType.DMA((blocks,))],
+    layer_out, grad_gate, grad_q, local_k, local_v = call(
+        backward_kernel, "backward", [half, half, half, full, full],
+        held_q, held_k, held_v, grad, attn, base_k, base_v, table, weights, front,
+        layer_out, grad_gate, hbm_out=2, scratch=[pltpu.SemaphoreType.DMA((2,))],
     )
     keep, sent = call(
         partial(suffix_kernel, n_chip), "suffix", [piece, piece], got, second, totals, chips
     )
     got = lax.ppermute(sent, "ctx", pairs)
-    grad_k, grad_v = call(
-        finish_kernel, "finish", [half, half],
-        held_k, held_v, local_k, local_v, keep, got, sums, turned, hbm_out=2,
+    grad_k, grad_v, grad_q = call(
+        finish_kernel, "finish", [half, half, half],
+        held_k, held_v, local_k, local_v, keep, got, sums, turned, grad_q, hbm_out=3,
         scratch=[
             pltpu.VMEM((length, HEAD_DIM), bf16), pltpu.VMEM((length, HEAD_DIM), bf16),
-            pltpu.SemaphoreType.DMA((2 * blocks,)),
+            pltpu.SemaphoreType.DMA((2 * blocks + 1,)),
         ],
     )
     return layer_out, grad_q, grad_k, grad_v, grad_gate

time: 98.4 us -> 97.3 us (0.989)
  Pallas kernels: 9.77 us -> 8.4 us
    pallas_call x13, Pallas kernels: 9.77 us -> 8.4 us  [call(): pl.pallas_call(kernel, out_shape=shapes, in_specs=[pl.BlockSpec(memory_sp...]
  transfers between devices with their start and end apart: 4 -> 4, of which waited for: 1 -> 2; matrix products, arithmetic and copies ran while one was open for 0% -> 0% of each run, Pallas kernels for 5% -> 4%
where the time goes in v5:
time: 97.3 us; the launch traced here: 96.9 us
  blocking collectives  59.9 us (62%)
  starting transfers between devices  27.1 us (28%)
  Pallas kernels  8.4 us (9%)
    all_to_all x4, blocking collectives, exchange(): return lax.all_to_all(x, axis, 0, 0, axis_index_groups=groups)  59.9 us
    ppermute x4, starting transfers between devices, on_device(): got = lax.ppermute(sent, 'ctx', pairs)  27.1 us
    pallas_call x13, Pallas kernels, call(): pl.pallas_call(kernel, out_shape=shapes, in_specs=[pl.BlockSpec(memory_sp...  8.4 us
  transfers between devices with their start and end apart: 4, of which 2 were waited for; matrix products, arithmetic and copies ran while one was open for 0% of the time, Pallas kernels for 4%

profile of v5, /device:TPU:1, one launch (start us, length us, event | category | flops | bytes accessed | tf_op | source)
XLA Modules:
  0.0 96.9 jit_solution(16326572509355237324)
XLA Ops:
  0.6 0.0 copy-start
  0.6 0.0 copy-start.1
  0.7 2.1 %states.1 = (f32[72,128]{1,0:T(8,128)S(1)}, f32[72,128]{1,0:T(8,128)S(1)}, f32[1,128,128]{2,1,0:T(8,128)S(1)}, f32[8,128]{1,0:T(8,128)S(1)}, f32[128,32]{1,0:T(8...) custom-call(bf16[1024,128]{1,0:T(8,128)(2,1)} %k_hbm.1, ...), custom_call_target="tpu_custom_call" | custom-call | flops 10000000 | bytes 10000000 | tf_op jit(solution)/shard_map/states/pallas_call | solution.py:419
  2.7 16.0 %collective-permute-start = (f32[72,128]{1,0:T(8,128)S(1)}, f32[72,128]{1,0:T(8,128)S(1)}, u32[]{:S(2)}, u32[]{:S(2)}) collective-permute-start(f32[72,128]{1,0:T(8,128)S(1)} %get-tuple-element.55), channel_id=1, source_target_pairs={{0,16},{16,0},{32,48},{48,32},{64,80},{80,64},{96,112},{112,96},{1... | collective-permute-start | bytes 110600 | tf_op jit(solution)/shard_map/ppermute | solution.py:463
  18.7 1.0 %local.1 = (f32[1024,128]{1,0:T(8,128)S(1)}, f32[1024,512]{1,0:T(8,128)S(1)}, bf16[1024,512]{1,0:T(8,128)(2,1)S(1)}) custom-call(bf16[1024,128]{1,0:T(8,128)(2,1)S(1)} %get-tuple-element.48.q_ref, bf16[1024,128]{1,0:T(8,128)(2,1)S(1)} %get-tuple-element.49.k_ref, bf16[1024,128]{1,0:T(8,128)(2,1)S(1)} %get-tuple-element.50.v_ref, ...), custom_call_target="tpu_custom_call" | custom-call | flops 2000000 | bytes 2000000 | tf_op jit(solution)/shard_map/local/pallas_call | solution.py:419
  19.7 0.0 collective-permute-done.got_ref
  19.8 15.1 %all_to_all.20.got_ref = f32[8,72,128]{2,1,0:T(8,128)S(1)} all-to-all(f32[8,72,128]{2,1,0:T(8,128)S(1)} %get-tuple-element.56), channel_id=1, replica_groups={{0,32,64,96,128,160,192,224},{16,48,80,112,144,176,208,240},{1,33,65,97..., dimensions={0} | all-to-all | bytes 589824 | tf_op jit(solution)/shard_map/all_to_all | solution.py:432
  34.9 0.1 prefix.1
  34.9 2.7 %collective-permute-start.1 = (f32[64,128]{1,0:T(8,128)S(1)}, f32[64,128]{1,0:T(8,128)S(1)}, u32[]{:S(2)}, u32[]{:S(2)}) collective-permute-start(f32[64,128]{1,0:T(8,128)S(1)} %get-tuple-element.60), channel_id=1, source_target_pairs={{0,16},{16,0},{32,48},{48,32},{64,80},{80,64},{96,112},{112,96},{1... | collective-permute-start | bytes 98312 | tf_op jit(solution)/shard_map/ppermute | solution.py:482
  37.7 0.5 gate.1
  38.2 0.3 collective-permute-done.1.got_ref
  38.5 0.6 attn.1
  39.1 6.7 %all_to_all.21.got_ref = f32[4,16,128]{2,1,0:T(8,128)S(1)} all-to-all(f32[4,16,128]{2,1,0:T(8,128)S(1)} %get-tuple-element.65), channel_id=1, replica_groups=mesh['section'=4,'ctx'=16,'exp'=16] {'section'}, dimensions={0} | all-to-all | bytes 65536 | tf_op jit(solution)/shard_map/all_to_all | solution.py:432
  45.8 23.4 %all_to_all.22.got_ref = f32[16,16,128]{2,1,0:T(8,128)S(1)} all-to-all(f32[16,16,128]{2,1,0:T(8,128)S(1)} %relay.1), channel_id=1, replica_groups=mesh['section'=4,'ctx'=16,'exp'=16] {'exp'}, dimensions={0} | all-to-all | bytes 262144 | tf_op jit(solution)/shard_map/all_to_all | solution.py:432
  69.2 0.9 grad.1
  70.1 5.9 %collective-permute-start.2 = (f32[64,128]{1,0:T(8,128)S(1)}, f32[64,128]{1,0:T(8,128)S(1)}, u32[]{:S(2)}, u32[]{:S(2)}) collective-permute-start(f32[64,128]{1,0:T(8,128)S(1)} %get-tuple-element.80), channel_id=1, source_target_pairs={{0,16},{16,0},{32,48},{48,32},{64,80},{80,64},{96,112},{112,96},{1... | collective-permute-start | bytes 98312 | tf_op jit(solution)/shard_map/ppermute | solution.py:499
  76.0 0.4 output.1
  76.5 0.4 collective-permute-done.2.got_ref
  76.9 14.8 %all_to_all.23.got_ref = f32[8,64,128]{2,1,0:T(8,128)S(1)} all-to-all(f32[8,64,128]{2,1,0:T(8,128)S(1)} %get-tuple-element.81), channel_id=1, replica_groups={{0,32,64,96,128,160,192,224},{16,48,80,112,144,176,208,240},{1,33,65,97..., dimensions={0} | all-to-all | bytes 524288 | tf_op jit(solution)/shard_map/all_to_all | solution.py:432
  91.7 0.1 suffix.1
  91.7 2.4 %collective-permute-start.3 = (f32[64,128]{1,0:T(8,128)S(1)}, f32[64,128]{1,0:T(8,128)S(1)}, u32[]{:S(2)}, u32[]{:S(2)}) collective-permute-start(f32[64,128]{1,0:T(8,128)S(1)} %get-tuple-element.85), channel_id=1, source_target_pairs={{0,16},{16,0},{32,48},{48,32},{64,80},{80,64},{96,112},{112,96},{1... | collective-permute-start | bytes 98312 | tf_op jit(solution)/shard_map/ppermute | solution.py:518
  94.1 1.6 %backward.1 = (bf16[1024,128]{1,0:T(8,128)(2,1)}, bf16[1024,128]{1,0:T(8,128)(2,1)}, bf16[1024,128]{1,0:T(8,128)(2,1)S(1)}, f32[1024,128]{1,0:T(8,128)S(1)}, f32[1024,128]{1,0:T(8,128)S(1)}) custom-call(bf16[1024,128]{1,0:T(8,128)(2,1)S(1)} %get-tuple-element.48.q_ref, bf16[1024,128]{1,0:T(8,128)(2,1)S(1)} %get-tuple-element.49.k_ref, ...), custom_call_target="tpu_custom_call" | custom-call | flops 2000000 | bytes 2000000 | tf_op jit(solution)/shard_map/backward/pallas_call | solution.py:419
  95.7 0.0 collective-permute-done.3.got_ref
  95.7 1.2 %finish.1 = (bf16[1024,128]{1,0:T(8,128)(2,1)}, bf16[1024,128]{1,0:T(8,128)(2,1)}, bf16[1024,128]{1,0:T(8,128)(2,1)}) custom-call(bf16[1024,128]{1,0:T(8,128)(2,1)S(1)} %get-tuple-element.49.k_ref, bf16[1024,128]{1,0:T(8,128)(2,1)S(1)} %get-tuple-element.50.v_ref, f32[1024,128]{1,0:T(8,128)S(1)} %get-tuple-element.77.gk_ref, ...), custom_call_target="tpu_custom_call" | custom-call | flops 2000000 | bytes 2000000 | tf_op jit(solution)/shard_map/finish/pallas_call | solution.py:419
  (5 shorter events, 0.1 us)
Async XLA Ops:
  0.6 37.0 %copy-start = (bf16[1024,128]{1,0:T(8,128)(2,1)S(1)}, bf16[1024,128]{1,0:T(8,128)(2,1)}, u32[]{:S(2)}) copy-start(bf16[1024,128]{1,0:T(8,128)(2,1)} %gin_ref.1) | copy-start | bytes 786436
  0.6 37.0 %copy-start.1 = (bf16[1024,128]{1,0:T(8,128)(2,1)S(1)}, bf16[1024,128]{1,0:T(8,128)(2,1)}, u32[]{:S(2)}) copy-start(bf16[1024,128]{1,0:T(8,128)(2,1)} %gout_ref.1) | copy-start | bytes 786436
  2.7 17.0 %collective-permute-start = (f32[72,128]{1,0:T(8,128)S(1)}, f32[72,128]{1,0:T(8,128)S(1)}, u32[]{:S(2)}, u32[]{:S(2)}) collective-permute-start(f32[72,128]{1,0:T(8,128)S(1)} %get-tuple-element.55), channel_id=1, source_target_pairs={{0,16},{16,0},{32,48},{48,32},{64,80},{80,64},{96,112},{112,96},{1... | collective-permute-start | bytes 110600 | tf_op jit(solution)/shard_map/ppermute | solution.py:463
  34.9 3.6 %collective-permute-start.1 = (f32[64,128]{1,0:T(8,128)S(1)}, f32[64,128]{1,0:T(8,128)S(1)}, u32[]{:S(2)}, u32[]{:S(2)}) collective-permute-start(f32[64,128]{1,0:T(8,128)S(1)} %get-tuple-element.60), channel_id=1, source_target_pairs={{0,16},{16,0},{32,48},{48,32},{64,80},{80,64},{96,112},{112,96},{1... | collective-permute-start | bytes 98312 | tf_op jit(solution)/shard_map/ppermute | solution.py:482
  70.1 6.8 %collective-permute-start.2 = (f32[64,128]{1,0:T(8,128)S(1)}, f32[64,128]{1,0:T(8,128)S(1)}, u32[]{:S(2)}, u32[]{:S(2)}) collective-permute-start(f32[64,128]{1,0:T(8,128)S(1)} %get-tuple-element.80), channel_id=1, source_target_pairs={{0,16},{16,0},{32,48},{48,32},{64,80},{80,64},{96,112},{112,96},{1... | collective-permute-start | bytes 98312 | tf_op jit(solution)/shard_map/ppermute | solution.py:499
  91.7 4.0 %collective-permute-start.3 = (f32[64,128]{1,0:T(8,128)S(1)}, f32[64,128]{1,0:T(8,128)S(1)}, u32[]{:S(2)}, u32[]{:S(2)}) collective-permute-start(f32[64,128]{1,0:T(8,128)S(1)} %get-tuple-element.85), channel_id=1, source_target_pairs={{0,16},{16,0},{32,48},{48,32},{64,80},{80,64},{96,112},{112,96},{1... | collective-permute-start | bytes 98312 | tf_op jit(solution)/shard_map/ppermute | solution.py:518

commit v6 on v5

--- a/solution.py
+++ b/solution.py
@@ -325,7 +325,7 @@
 
 def output_kernel(
     attn_ref, aux_ref, gin_ref, gain_ref, gout_ref, k_ref, v_ref, turned_ref,
-    layer_ref, gate_ref, base_k_ref, base_v_ref,
+    weights_ref, grad_ref, layer_ref, gate_ref, base_k_ref, gv_ref, tail_ref,
 ):
     length = gout_ref.shape[0]
     both = aux_ref[aux_ref.shape[0] - HEAD_DIM :, :16]
@@ -337,17 +337,28 @@
         layer_ref[rows, :] = layer.astype(bf16)
         gate_ref[rows, :] = (gout_ref[rows, :].astype(f32) * layer * (1.0 - prob)).astype(bf16)
     turned = turned_ref[...]
-    for b in range(length // BLOCK - 1):
-        rows = slice(b * BLOCK, (b + 1) * BLOCK)
-        tail = column(turned, b * BLOCK, BLOCK, 2)
+    blocks = length // BLOCK
+    for b in range(blocks):
+        at = b * BLOCK
         later = aux_ref[b * HEAD_DIM : (b + 1) * HEAD_DIM, :]
-        base_k_ref[rows, :] = tail * exact_dot(v_ref[rows, :], later, True)
-        base_v_ref[rows, :] = tail * exact_dot(k_ref[rows, :], later)
+        for i in range(BLOCK // TILE):
+            first = at + i * TILE
+            rows = slice(first, first + TILE)
+            tail = jnp.broadcast_to(column(turned, first, TILE, 2), (TILE, HEAD_DIM))
+            tail_ref[rows, :] = tail
+            add_v = dot(weights_ref[rows, : (i + 1) * TILE], grad_ref[rows, :], 0, 0)
+            more_v = 0.0
+            if b < blocks - 1:
+                base_k_ref[rows, :] = tail * exact_dot(v_ref[rows, :], later, True)
+                more_v = tail * exact_dot(k_ref[rows, :], later)
+            if i:
+                gv_ref[at:first, :] += add_v[: i * TILE, :]
+            gv_ref[rows, :] = add_v[i * TILE :, :] + more_v
 
 
 def backward_kernel(
-    q_ref, k_ref, v_ref, grad_ref, attn_ref, base_k_ref, base_v_ref, table_ref, weights_ref, front_ref,
-    layer_ref, gate_ref, layer_hbm, gate_hbm, gq_ref, gk_ref, gv_ref, sems,
+    q_ref, k_ref, v_ref, grad_ref, attn_ref, base_k_ref, table_ref, front_ref,
+    layer_ref, gate_ref, layer_hbm, gate_hbm, gq_ref, gk_ref, sems,
 ):
     length = q_ref.shape[0]
     blocks = length // BLOCK
@@ -364,31 +375,27 @@
             rows = slice(at + i * TILE, at + (i + 1) * TILE)
             cols = slice(at, at + (i + 1) * TILE)
             q, g = q_ref[rows, :], grad_ref[rows, :]
-            wq = weights_ref[rows, : (i + 1) * TILE]
             table = table_ref[rows, : (i + 1) * TILE]
             gw = (dot(g, v_ref[cols, :], 1, 1) * table).astype(bf16)
             grad_q = dot(gw, k_ref[cols, :]) + front_ref[rows, :] * exact_dot(g, entering, True)
             gq_ref[rows, :] = grad_q.astype(bf16)
-            add_k, add_v = dot(gw, q, 0, 0), dot(wq, g, 0, 0)
+            add_k = dot(gw, q, 0, 0)
             more_k = base_k_ref[rows, :] if b < blocks - 1 else 0.0
-            more_v = base_v_ref[rows, :] if b < blocks - 1 else 0.0
             if i:
                 old = slice(at, at + i * TILE)
                 gk_ref[old, :] += add_k[: i * TILE, :]
-                gv_ref[old, :] += add_v[: i * TILE, :]
             gk_ref[rows, :] = add_k[i * TILE :, :] + more_k
-            gv_ref[rows, :] = add_v[i * TILE :, :] + more_v
     for copy in copies:
         copy.wait()
 
 
 def finish_kernel(
-    k_ref, v_ref, gk_ref, gv_ref, keep_ref, got_ref, sums_ref, turned_ref, gq_ref,
+    k_ref, v_ref, gk_ref, gv_ref, keep_ref, got_ref, sums_ref, tail_ref, gq_ref,
     ok_hbm, ov_hbm, oq_hbm, ok_ref, ov_ref, sems,
 ):
     length = k_ref.shape[0]
     blocks = length // BLOCK
-    sums, turned = sums_ref[...], turned_ref[...]
+    sums = sums_ref[...]
     start = whole_state(keep_ref, got_ref)
     after = jnp.zeros((1, 1), f32)
     copies = [pltpu.make_async_copy(gq_ref, oq_hbm, sems.at[2 * blocks])]
@@ -396,7 +403,7 @@
     for b in reversed(range(blocks)):
         at = b * BLOCK
         rows = slice(at, at + BLOCK)
-        tail = column(turned, at, BLOCK, 2)
+        tail = tail_ref[rows, :]
         state = start * jnp.exp(after)
         after = after + last_of(sums, b)
         part = pl.ds(at, BLOCK)
@@ -498,18 +505,18 @@
     )
     got = lax.ppermute(sent, "ctx", pairs)
     early = ((length - BLOCK, HEAD_DIM), f32)
-    layer_out, grad_gate, base_k, base_v = call(
-        output_kernel, "output", [half, half, early, early],
-        attn, aux, gate_input, gain, grad_output, held_k, held_v, turned,
+    layer_out, grad_gate, base_k, local_v, tail = call(
+        output_kernel, "output", [half, half, early, full, full],
+        attn, aux, gate_input, gain, grad_output, held_k, held_v, turned, weights, grad,
     )
     sent, second = call(
         partial(back_pair_kernel, n_chip), "back_pair",
-        [((n_chip, part, HEAD_DIM), f32), piece], keep, got, totals, base_v, hbm_last=True,
+        [((n_chip, part, HEAD_DIM), f32), piece], keep, got, totals, base_k, hbm_last=True,
     )
     got = exchange(sent, "ctx", lines)
-    layer_out, grad_gate, grad_q, local_k, local_v = call(
-        backward_kernel, "backward", [half, half, half, full, full],
-        held_q, held_k, held_v, grad, attn, base_k, base_v, table, weights, front,
+    layer_out, grad_gate, grad_q, local_k = call(
+        backward_kernel, "backward", [half, half, half, full],
+        held_q, held_k, held_v, grad, attn, base_k, table, front,
         layer_out, grad_gate, hbm_out=2, scratch=[pltpu.SemaphoreType.DMA((2,))],
     )
     keep, sent = call(
@@ -518,7 +525,7 @@
     got = lax.ppermute(sent, "ctx", pairs)
     grad_k, grad_v, grad_q = call(
         finish_kernel, "finish", [half, half, half],
-        held_k, held_v, local_k, local_v, keep, got, sums, turned, grad_q, hbm_out=3,
+        held_k, held_v, local_k, local_v, keep, got, sums, tail, grad_q, hbm_out=3,
         scratch=[
             pltpu.VMEM((length, HEAD_DIM), bf16), pltpu.VMEM((length, HEAD_DIM), bf16),
             pltpu.SemaphoreType.DMA((2 * blocks + 1,)),

time: 97.3 us -> 97 us (level)
  transfers between devices with their start and end apart: 4 -> 4, of which waited for: 2 -> 1; matrix products, arithmetic and copies ran while one was open for 0% -> 0% of each run, Pallas kernels for 4% -> 4%
where the time goes in v6:
time: 97 us; the launch traced here: 96.6 us
  blocking collectives  59.9 us (62%)
  starting transfers between devices  27.1 us (28%)
  Pallas kernels  8.49 us (9%)
    all_to_all x4, blocking collectives, exchange(): return lax.all_to_all(x, axis, 0, 0, axis_index_groups=groups)  59.9 us
    ppermute x4, starting transfers between devices, on_device(): got = lax.ppermute(sent, 'ctx', pairs)  27.1 us
    pallas_call x13, Pallas kernels, call(): pl.pallas_call(kernel, out_shape=shapes, in_specs=[pl.BlockSpec(memory_sp...  8.49 us
  transfers between devices with their start and end apart: 4, of which 1 were waited for; matrix products, arithmetic and copies ran while one was open for 0% of the time, Pallas kernels for 4%

profile of v6, /device:TPU:1, one launch (start us, length us, event | category | flops | bytes accessed | tf_op | source)
XLA Modules:
  0.0 96.6 jit_solution(1302145057857770381)
XLA Ops:
  0.6 0.0 copy-start
  0.6 0.0 copy-start.1
  0.7 2.1 %states.1 = (f32[72,128]{1,0:T(8,128)S(1)}, f32[72,128]{1,0:T(8,128)S(1)}, f32[1,128,128]{2,1,0:T(8,128)S(1)}, f32[8,128]{1,0:T(8,128)S(1)}, f32[128,32]{1,0:T(8...) custom-call(bf16[1024,128]{1,0:T(8,128)(2,1)} %k_hbm.1, ...), custom_call_target="tpu_custom_call" | custom-call | flops 10000000 | bytes 10000000 | tf_op jit(solution)/shard_map/states/pallas_call | solution.py:426
  2.7 16.0 %collective-permute-start = (f32[72,128]{1,0:T(8,128)S(1)}, f32[72,128]{1,0:T(8,128)S(1)}, u32[]{:S(2)}, u32[]{:S(2)}) collective-permute-start(f32[72,128]{1,0:T(8,128)S(1)} %get-tuple-element.55), channel_id=1, source_target_pairs={{0,16},{16,0},{32,48},{48,32},{64,80},{80,64},{96,112},{112,96},{1... | collective-permute-start | bytes 110600 | tf_op jit(solution)/shard_map/ppermute | solution.py:470
  18.7 1.0 %local.1 = (f32[1024,128]{1,0:T(8,128)S(1)}, f32[1024,512]{1,0:T(8,128)S(1)}, bf16[1024,512]{1,0:T(8,128)(2,1)S(1)}) custom-call(bf16[1024,128]{1,0:T(8,128)(2,1)S(1)} %get-tuple-element.48.q_ref, bf16[1024,128]{1,0:T(8,128)(2,1)S(1)} %get-tuple-element.49.k_ref, bf16[1024,128]{1,0:T(8,128)(2,1)S(1)} %get-tuple-element.50.v_ref, ...), custom_call_target="tpu_custom_call" | custom-call | flops 2000000 | bytes 2000000 | tf_op jit(solution)/shard_map/local/pallas_call | solution.py:426
  19.7 0.0 collective-permute-done.got_ref
  19.8 15.1 %all_to_all.20.got_ref = f32[8,72,128]{2,1,0:T(8,128)S(1)} all-to-all(f32[8,72,128]{2,1,0:T(8,128)S(1)} %get-tuple-element.56), channel_id=1, replica_groups={{0,32,64,96,128,160,192,224},{16,48,80,112,144,176,208,240},{1,33,65,97..., dimensions={0} | all-to-all | bytes 589824 | tf_op jit(solution)/shard_map/all_to_all | solution.py:439
  34.9 0.1 prefix.1
  34.9 2.7 %collective-permute-start.1 = (f32[64,128]{1,0:T(8,128)S(1)}, f32[64,128]{1,0:T(8,128)S(1)}, u32[]{:S(2)}, u32[]{:S(2)}) collective-permute-start(f32[64,128]{1,0:T(8,128)S(1)} %get-tuple-element.60), channel_id=1, source_target_pairs={{0,16},{16,0},{32,48},{48,32},{64,80},{80,64},{96,112},{112,96},{1... | collective-permute-start | bytes 98312 | tf_op jit(solution)/shard_map/ppermute | solution.py:489
  37.7 0.5 gate.1
  38.2 0.3 collective-permute-done.1.got_ref
  38.5 0.6 attn.1
  39.1 6.7 %all_to_all.21.got_ref = f32[4,16,128]{2,1,0:T(8,128)S(1)} all-to-all(f32[4,16,128]{2,1,0:T(8,128)S(1)} %get-tuple-element.65), channel_id=1, replica_groups=mesh['section'=4,'ctx'=16,'exp'=16] {'section'}, dimensions={0} | all-to-all | bytes 65536 | tf_op jit(solution)/shard_map/all_to_all | solution.py:439
  45.7 23.4 %all_to_all.22.got_ref = f32[16,16,128]{2,1,0:T(8,128)S(1)} all-to-all(f32[16,16,128]{2,1,0:T(8,128)S(1)} %relay.1), channel_id=1, replica_groups=mesh['section'=4,'ctx'=16,'exp'=16] {'exp'}, dimensions={0} | all-to-all | bytes 262144 | tf_op jit(solution)/shard_map/all_to_all | solution.py:439
  69.2 0.9 grad.1
  70.1 5.9 %collective-permute-start.2 = (f32[64,128]{1,0:T(8,128)S(1)}, f32[64,128]{1,0:T(8,128)S(1)}, u32[]{:S(2)}, u32[]{:S(2)}) collective-permute-start(f32[64,128]{1,0:T(8,128)S(1)} %get-tuple-element.79), channel_id=1, source_target_pairs={{0,16},{16,0},{32,48},{48,32},{64,80},{80,64},{96,112},{112,96},{1... | collective-permute-start | bytes 98312 | tf_op jit(solution)/shard_map/ppermute | solution.py:506
  76.0 0.8 output.1
  76.9 0.0 collective-permute-done.2.got_ref
  76.9 14.8 %all_to_all.23.got_ref = f32[8,64,128]{2,1,0:T(8,128)S(1)} all-to-all(f32[8,64,128]{2,1,0:T(8,128)S(1)} %get-tuple-element.80), channel_id=1, replica_groups={{0,32,64,96,128,160,192,224},{16,48,80,112,144,176,208,240},{1,33,65,97..., dimensions={0} | all-to-all | bytes 524288 | tf_op jit(solution)/shard_map/all_to_all | solution.py:439
  91.7 0.1 suffix.1
  91.7 2.4 %collective-permute-start.3 = (f32[64,128]{1,0:T(8,128)S(1)}, f32[64,128]{1,0:T(8,128)S(1)}, u32[]{:S(2)}, u32[]{:S(2)}) collective-permute-start(f32[64,128]{1,0:T(8,128)S(1)} %get-tuple-element.84), channel_id=1, source_target_pairs={{0,16},{16,0},{32,48},{48,32},{64,80},{80,64},{96,112},{112,96},{1... | collective-permute-start | bytes 98312 | tf_op jit(solution)/shard_map/ppermute | solution.py:525
  94.1 1.3 %backward.1 = (bf16[1024,128]{1,0:T(8,128)(2,1)}, bf16[1024,128]{1,0:T(8,128)(2,1)}, bf16[1024,128]{1,0:T(8,128)(2,1)S(1)}, f32[1024,128]{1,0:T(8,128)S(1)}) custom-call(bf16[1024,128]{1,0:T(8,128)(2,1)S(1)} %get-tuple-element.48.q_ref, bf16[1024,128]{1,0:T(8,128)(2,1)S(1)} %get-tuple-element.49.k_ref, bf16[1024,128]{1,0:T(8,128)(2,1)S(1)} %get-tuple-element.50.v_ref, ...), custom_call_target="tpu_custom_call" | custom-call | flops 2000000 | bytes 2000000 | tf_op jit(solution)/shard_map/backward/pallas_call | solution.py:426
  95.4 0.0 collective-permute-done.3.got_ref
  95.4 1.2 %finish.1 = (bf16[1024,128]{1,0:T(8,128)(2,1)}, bf16[1024,128]{1,0:T(8,128)(2,1)}, bf16[1024,128]{1,0:T(8,128)(2,1)}) custom-call(bf16[1024,128]{1,0:T(8,128)(2,1)S(1)} %get-tuple-element.49.k_ref, bf16[1024,128]{1,0:T(8,128)(2,1)S(1)} %get-tuple-element.50.v_ref, f32[1024,128]{1,0:T(8,128)S(1)} %get-tuple-element.76.gk_ref, ...), custom_call_target="tpu_custom_call" | custom-call | flops 2000000 | bytes 2000000 | tf_op jit(solution)/shard_map/finish/pallas_call | solution.py:426
  (5 shorter events, 0.1 us)
Async XLA Ops:
  0.6 37.0 %copy-start = (bf16[1024,128]{1,0:T(8,128)(2,1)S(1)}, bf16[1024,128]{1,0:T(8,128)(2,1)}, u32[]{:S(2)}) copy-start(bf16[1024,128]{1,0:T(8,128)(2,1)} %gin_ref.1) | copy-start | bytes 786436
  0.6 37.0 %copy-start.1 = (bf16[1024,128]{1,0:T(8,128)(2,1)S(1)}, bf16[1024,128]{1,0:T(8,128)(2,1)}, u32[]{:S(2)}) copy-start(bf16[1024,128]{1,0:T(8,128)(2,1)} %gout_ref.1) | copy-start | bytes 786436
  2.7 17.0 %collective-permute-start = (f32[72,128]{1,0:T(8,128)S(1)}, f32[72,128]{1,0:T(8,128)S(1)}, u32[]{:S(2)}, u32[]{:S(2)}) collective-permute-start(f32[72,128]{1,0:T(8,128)S(1)} %get-tuple-element.55), channel_id=1, source_target_pairs={{0,16},{16,0},{32,48},{48,32},{64,80},{80,64},{96,112},{112,96},{1... | collective-permute-start | bytes 110600 | tf_op jit(solution)/shard_map/ppermute | solution.py:470
  34.9 3.6 %collective-permute-start.1 = (f32[64,128]{1,0:T(8,128)S(1)}, f32[64,128]{1,0:T(8,128)S(1)}, u32[]{:S(2)}, u32[]{:S(2)}) collective-permute-start(f32[64,128]{1,0:T(8,128)S(1)} %get-tuple-element.60), channel_id=1, source_target_pairs={{0,16},{16,0},{32,48},{48,32},{64,80},{80,64},{96,112},{112,96},{1... | collective-permute-start | bytes 98312 | tf_op jit(solution)/shard_map/ppermute | solution.py:489
  70.1 6.8 %collective-permute-start.2 = (f32[64,128]{1,0:T(8,128)S(1)}, f32[64,128]{1,0:T(8,128)S(1)}, u32[]{:S(2)}, u32[]{:S(2)}) collective-permute-start(f32[64,128]{1,0:T(8,128)S(1)} %get-tuple-element.79), channel_id=1, source_target_pairs={{0,16},{16,0},{32,48},{48,32},{64,80},{80,64},{96,112},{112,96},{1... | collective-permute-start | bytes 98312 | tf_op jit(solution)/shard_map/ppermute | solution.py:506
  91.7 3.7 %collective-permute-start.3 = (f32[64,128]{1,0:T(8,128)S(1)}, f32[64,128]{1,0:T(8,128)S(1)}, u32[]{:S(2)}, u32[]{:S(2)}) collective-permute-start(f32[64,128]{1,0:T(8,128)S(1)} %get-tuple-element.84), channel_id=1, source_target_pairs={{0,16},{16,0},{32,48},{48,32},{64,80},{80,64},{96,112},{112,96},{1... | collective-permute-start | bytes 98312 | tf_op jit(solution)/shard_map/ppermute | solution.py:525
